TPU v7x, 128 devices: a whole 4x4x4 slice. The times are simulated.
128 devices in a mesh: fsdp: 4 (over z), seq: 32 (over x, y, core).
Axes of the slice: x: 4, y: 4, z: 4, core: 2. Of those that a mesh axis runs over, the one named last changes fastest.
Arguments:
- queries: bfloat16 [4, 8192, 2048], P('fsdp', 'seq'), may hold values from -32 to 32
- keys: bfloat16 [4, 8192, 2048], P('fsdp', 'seq'), may hold values from -6 to 6
- values: bfloat16 [4, 8192, 2048], P('fsdp', 'seq'), may hold values from -6 to 6
- out_grad: bfloat16 [4, 8192, 2048], P('fsdp', 'seq'), may hold values from -6 to 6
- out_weight: bfloat16 [2048, 2048], P('fsdp'), may hold values from -0.125 to 0.125
- key_blocks: int32 [4, 64, 10], P('fsdp'), may hold values from 0 to 63, as said below
- block_counts: int32 [4, 64], P('fsdp'), may hold values from 2 to 10, as said below
Outputs:
- query_grad: bfloat16 [4, 8192, 2048], P('fsdp', 'seq')
- key_grad: bfloat16 [4, 8192, 2048], P('fsdp', 'seq')
- value_grad: bfloat16 [4, 8192, 2048], P('fsdp', 'seq')
- wo_grad: float32 [2048, 2048], P('fsdp')
Inputs may be any that keep to these rules, and one draw needn't show every extreme that they name: `key_blocks`: within a row the numbers are distinct; slots 0, 1 and 2 hold blocks i, i + 1 and i - 1 modulo 64; slots at or past the row's count are ignored. `block_counts`: every sample has a query block whose count is 10.
All inputs are finite; a program needn't handle non-finite values.
Results may differ from a plain program's by a relative error of at most 0.025.
Values may be sent and summed in bfloat16 or wider, within the bound.
A program may use at most 128 MiB of HBM per device.

v0:
```python
import jax
import jax.numpy as jnp
from jax import lax
from jax.sharding import PartitionSpec as P

HEADS = 32
HD = 64
BLK = 128
MAXK = 10


NEG_FILL = -1e30


def pair_scores(query_blocks, chosen):
    return jnp.einsum(
        "iqhd,ikhd->ihqk", query_blocks, chosen, preferred_element_type=jnp.float32
    ) * HD ** (-0.5)


def blocked(array):
    return array.reshape(-1, BLK, array.shape[1], HD)


def head_forward(query_h, key_h, value_h, adjacency, slot_live):
    query_blocks = blocked(query_h)
    key_heads = blocked(key_h)
    value_heads = blocked(value_h)
    blocks_total = query_blocks.shape[0]
    head_count = query_blocks.shape[2]

    def stat_step(carried, slot):
        row_max, row_sum = carried
        score = pair_scores(query_blocks, key_heads[adjacency[:, slot]])
        usable = slot_live[:, slot][:, None, None, None]
        score = jnp.where(usable, score, NEG_FILL)
        new_max = jnp.maximum(row_max, jnp.max(score, axis=-1))
        expo = jnp.where(usable, jnp.exp(score - new_max[..., None]), 0.0)
        row_sum = row_sum * jnp.exp(row_max - new_max) + jnp.sum(expo, axis=-1)
        return ((new_max, row_sum), None)

    start_max = jnp.full((blocks_total, head_count, BLK), NEG_FILL, jnp.float32)
    start_sum = jnp.zeros((blocks_total, head_count, BLK), jnp.float32)
    (row_max, row_sum), _ = lax.scan(stat_step, (start_max, start_sum), jnp.arange(MAXK))

    def output_step(accum, slot):
        picked = adjacency[:, slot]
        score = pair_scores(query_blocks, key_heads[picked])
        usable = slot_live[:, slot][:, None, None, None]
        prob_half = jnp.where(
            usable, jnp.exp(score - row_max[..., None]) / row_sum[..., None], 0.0
        ).astype(jnp.bfloat16)
        accum = accum + jnp.einsum(
            "ihqk,ikhd->iqhd", prob_half, value_heads[picked], preferred_element_type=jnp.float32
        )
        return (accum, None)

    start_out = jnp.zeros(query_blocks.shape, jnp.float32)
    accum, _ = lax.scan(output_step, start_out, jnp.arange(MAXK))
    return (row_max, row_sum, accum.astype(jnp.bfloat16))


def head_backward(
    query_h, key_h, value_h, grad_h, row_max, row_sum, attn_blocks, adjacency, slot_live
):
    query_blocks = blocked(query_h)
    key_heads = blocked(key_h)
    value_heads = blocked(value_h)
    grad_blocks = blocked(grad_h)
    scale_factor = HD ** (-0.5)
    row_dot = jnp.sum(
        grad_blocks.astype(jnp.float32) * attn_blocks.astype(jnp.float32), axis=-1
    ).transpose(0, 2, 1)

    def grad_step(carried, slot):
        query_accum, key_accum, value_accum = carried
        picked = adjacency[:, slot]
        chosen_keys = key_heads[picked]
        chosen_values = value_heads[picked]
        score = pair_scores(query_blocks, chosen_keys)
        usable = slot_live[:, slot][:, None, None, None]
        prob_full = jnp.where(usable, jnp.exp(score - row_max[..., None]) / row_sum[..., None], 0.0)
        prob_half = prob_full.astype(jnp.bfloat16)
        prob_grad = jnp.einsum(
            "iqhd,ikhd->ihqk", grad_blocks, chosen_values, preferred_element_type=jnp.float32
        )
        score_grad = (prob_full * (prob_grad - row_dot[..., None])).astype(jnp.bfloat16)
        query_accum = (
            query_accum
            + jnp.einsum(
                "ihqk,ikhd->iqhd", score_grad, chosen_keys, preferred_element_type=jnp.float32
            )
            * scale_factor
        )
        key_terms = (
            jnp.einsum(
                "ihqk,iqhd->ikhd", score_grad, query_blocks, preferred_element_type=jnp.float32
            )
            * scale_factor
        )
        value_terms = jnp.einsum(
            "ihqk,iqhd->ikhd", prob_half, grad_blocks, preferred_element_type=jnp.float32
        )
        key_accum = key_accum.at[picked].add(key_terms)
        value_accum = value_accum.at[picked].add(value_terms)
        return ((query_accum, key_accum, value_accum), None)

    zeros_start = jnp.zeros(query_blocks.shape, jnp.float32)
    (query_accum, key_accum, value_accum), _ = lax.scan(
        grad_step, (zeros_start, zeros_start, zeros_start), jnp.arange(MAXK)
    )
    head_count = query_h.shape[1]
    return tuple(
        (
            accum.astype(jnp.bfloat16).reshape(-1, head_count, HD)
            for accum in (query_accum, key_accum, value_accum)
        )
    )


def on_device(queries, keys, values, out_grad, out_weight, key_blocks, block_counts):
    local_tokens = queries.shape[1]
    model_width = queries.shape[2]
    seq_devices = lax.axis_size("seq")
    loss_grad = out_grad[0]
    adjacency = key_blocks[0]
    slot_live = jnp.arange(MAXK)[None, :] < block_counts[0][:, None]

    def head_groups(array):
        return array[0].reshape(local_tokens, seq_devices, HEADS // seq_devices, HD)

    attn_grad = lax.dot_general(
        loss_grad,
        lax.all_gather(out_weight, "fsdp", axis=0, tiled=True),
        (((1,), (1,)), ((), ())),
        preferred_element_type=jnp.float32,
    ).astype(jnp.bfloat16)

    def attend(heads_in):
        query_h, key_h, value_h, grad_h = (member[:, 0] for member in heads_in)
        row_max, row_sum, attn_blocks = head_forward(query_h, key_h, value_h, adjacency, slot_live)
        query_g, key_g, value_g = head_backward(
            query_h, key_h, value_h, grad_h, row_max, row_sum, attn_blocks, adjacency, slot_live
        )
        return (query_g, key_g, value_g, attn_blocks.reshape(-1, query_h.shape[1], HD))

    query_g, key_g, value_g, attn_heads = attend(
        (
            lax.all_to_all(head_groups(queries), "seq", split_axis=1, concat_axis=0, tiled=True),
            lax.all_to_all(head_groups(keys), "seq", split_axis=1, concat_axis=0, tiled=True),
            lax.all_to_all(head_groups(values), "seq", split_axis=1, concat_axis=0, tiled=True),
            lax.all_to_all(
                head_groups(attn_grad[None]), "seq", split_axis=1, concat_axis=0, tiled=True
            ),
        )
    )
    query_t, key_t, value_t, attn_t = (
        lax.all_to_all(query_g, "seq", split_axis=0, concat_axis=1, tiled=True),
        lax.all_to_all(key_g, "seq", split_axis=0, concat_axis=1, tiled=True),
        lax.all_to_all(value_g, "seq", split_axis=0, concat_axis=1, tiled=True),
        lax.all_to_all(attn_heads, "seq", split_axis=0, concat_axis=1, tiled=True),
    )
    attn_out = attn_t.reshape(local_tokens, model_width)
    share = lax.psum_scatter(
        lax.dot_general(
            attn_out, loss_grad, (((0,), (0,)), ((), ())), preferred_element_type=jnp.float32
        ),
        ("fsdp", "seq"),
        scatter_dimension=0,
        tiled=True,
    )
    wo_grad = lax.all_gather(share.astype(jnp.bfloat16), "seq", axis=0, tiled=True).astype(
        share.dtype
    )

    def to_tokens(array):
        return array.reshape(1, local_tokens, model_width)

    return (to_tokens(query_t), to_tokens(key_t), to_tokens(value_t), wo_grad)


def solution(mesh):
    return jax.shard_map(
        on_device,
        mesh=mesh,
        in_specs=(
            P("fsdp", "seq", None),
            P("fsdp", "seq", None),
            P("fsdp", "seq", None),
            P("fsdp", "seq", None),
            P("fsdp", None),
            P("fsdp", None, None),
            P("fsdp", None),
        ),
        out_specs=(
            P("fsdp", "seq", None),
            P("fsdp", "seq", None),
            P("fsdp", "seq", None),
            P("fsdp", None),
        ),
        check_vma=False,
    )
```

profile of v0, /device:TPU:1, one launch (start us, length us, event | category | flops | bytes accessed | tf_op | source)
XLA Modules:
  0.0 1820.3 jit_solution(2905158526303225540)
XLA Ops:
  9.6 8.6 all-to-all-start
  19.5 15.6 all-to-all-done
  41.3 14.6 all-to-all-done.1
  69.3 8.2 all-to-all-done.2
  82.6 123.3 %while.39 = (s32[]{:T(128)}, f32[64,1,128]{2,0,1:T(8,128)S(1)}, f32[64,1,128]{2,0,1:T(8,128)S(1)}, s32[10]{0:T(128)S(1)}, pred[64,10]{0,1:T(8,128)(4,1)S(1)}, /*...) while((s32[]{:T(128)}, f32[64,1,128]{2,0,1:T(8,128)S(1)}, ...), condition=%wide.region_3.4_spmd.clone, body=%wide.region_0.3_spmd.clone.sunk | while | flops 142648512 | bytes 13014454 | solution.py:44
  205.9 6.7 convolution_convert_fusion
  219.6 113.9 %while.40 = (s32[]{:T(128)}, f32[64,128,1,64]{1,3,0,2:T(8,128)}, s32[10]{0:T(128)S(1)}, s32[64,10]{0,1:T(8,128)S(1)}, bf16[64,128,1,64]{1,3,2,0:T(8,128)(2,1)S(1...) while((s32[]{:T(128)}, f32[64,128,1,64]{1,3,0,2:T(8,128)}, ...), condition=%wide.region_5.6_spmd.clone, body=%wide.region_4.5_spmd.clone.sunk | while | flops 274728128 | bytes 11605637 | solution.py:59
  236.3 5.6 bitcast_add_fusion.7
  247.7 5.6 bitcast_add_fusion.7
  259.2 5.6 bitcast_add_fusion.7
  270.7 5.6 bitcast_add_fusion.7
  282.1 5.6 bitcast_add_fusion.7
  293.6 5.6 bitcast_add_fusion.7
  305.0 5.6 bitcast_add_fusion.7
  316.5 5.6 bitcast_add_fusion.7
  328.0 5.6 bitcast_add_fusion.7
  356.1 24.5 %all_to_all.120 = bf16[32,2,8192]{2,1,0:T(2,128)(2,1)} all-to-all(bf16[32,2,8192]{2,1,0:T(2,128)(2,1)} %reshape.275), channel_id=1, replica_groups=mesh['fsdp'=4,'seq'=32] {'seq'}, dimensions={0} | all-to-all | bytes 2097152 | tf_op jit(solution)/shard_map/all_to_all | solution.py:161
  380.6 10.2 reshape.276
  390.8 8.9 copy.85
  401.7 8.1 fusion.19
  412.7 653.8 %reduce-scatter.2.cloned.1.call-done = f32[16,2048]{1,0:T(8,128)} async-done(((f32[2048,2048]{1,0:T(8,128)}), f32[16,2048]{1,0:T(8,128)}) %reduce-scatter.2.cloned.1.call-update) | async-done | bytes 131088 | tf_op jit(solution)/shard_map/reduce_scatter | solution.py:164
  1071.2 477.0 %while.41 = (s32[]{:T(128)}, f32[64,128,1,64]{1,3,0,2:T(8,128)}, f32[64,128,1,64]{1,3,0,2:T(8,128)}, f32[64,128,1,64]{1,3,0,2:T(8,128)}, s32[10]{0:T(128)S(1)}, ...) while((s32[]{:T(128)}, f32[64,128,1,64]{1,3,0,2:T(8,128)}, ...), condition=%wide.region_10.11_spmd.clone, body=%wide.region_7.10_spmd.clone.sunk | while | flops 682624192 | bytes 68262136 | solution.py:109
  1092.6 10.3 scatter_fusion
  1102.9 5.2 fusion.69
  1108.1 10.4 scatter_fusion.1
  1128.1 5.1 multiply_convert_fusion.2
  1140.5 10.4 scatter_fusion
  1155.9 10.4 scatter_fusion.1
  1175.9 5.1 multiply_convert_fusion.2
  1188.3 10.3 scatter_fusion
  1203.7 10.4 scatter_fusion.1
  1223.6 5.1 multiply_convert_fusion.2
  1236.0 10.3 scatter_fusion
  1251.4 10.3 scatter_fusion.1
  1283.7 10.3 scatter_fusion
  1299.1 10.3 scatter_fusion.1
  1319.1 5.1 multiply_convert_fusion.2
  1331.5 10.3 scatter_fusion
  1346.9 10.3 scatter_fusion.1
  1366.8 5.1 multiply_convert_fusion.2
  1379.2 10.4 scatter_fusion
  1394.7 10.3 scatter_fusion.1
  1414.6 5.1 multiply_convert_fusion.2
  1427.0 10.3 scatter_fusion
  1442.4 10.4 scatter_fusion.1
  1474.7 10.3 scatter_fusion
  1490.1 10.4 scatter_fusion.1
  1522.5 10.3 scatter_fusion
  1537.9 10.3 scatter_fusion.1
  1551.1 6.1 reshape.266
  1557.3 46.6 %reduce.5 = bf16[8192,64]{1,0:T(8,128)(2,1)} reduce(bf16[8192,1,64]{2,1,0:T(2,128)(2,1)} %reshape.266, bf16[]{:T(256)} %broadcast.181), dimensions={1}, to_apply=%reshape.266.reduce_sub_computation | reduce | bytes 2097154 | tf_op jit(solution)/shard_map/reshape | solution.py:115
  1608.7 12.5 all-to-all-start.4
  1622.5 6.1 reshape.267
  1628.6 46.4 %reduce.6 = bf16[8192,64]{1,0:T(8,128)(2,1)} reduce(bf16[8192,1,64]{2,1,0:T(2,128)(2,1)} %reshape.267, bf16[]{:T(256)} %broadcast.181), dimensions={1}, to_apply=%reshape.267.reduce_sub_computation | reduce | bytes 2097154 | tf_op jit(solution)/shard_map/reshape | solution.py:115
  1679.8 8.0 all-to-all-start.5
  1689.1 6.1 reshape.268
  1695.3 45.1 %reduce.7 = bf16[8192,64]{1,0:T(8,128)(2,1)S(1)} reduce(bf16[8192,1,64]{2,1,0:T(2,128)(2,1)} %reshape.268, bf16[]{:T(256)} %broadcast.181), dimensions={1}, to_apply=%reshape.268.reduce_sub_computation | reduce | bytes 2097154 | tf_op jit(solution)/shard_map/reshape | solution.py:115
  1742.7 7.8 all-to-all-start.6
  1750.5 10.2 reshape.270
  1760.6 8.2 copy.74
  1771.1 10.2 reshape.272
  1781.2 8.2 copy.78
  1791.7 7.0 reshape.274
  1798.6 8.2 copy.82
  (411 shorter events, 457.3 us)
Async XLA Ops:
  7.2 198.7 %copy-start = (bf16[1,256,2048]{2,1,0:T(8,128)(2,1)S(1)}, bf16[1,256,2048]{2,1,0:T(8,128)(2,1)}, u32[]{:S(2)}) copy-start(bf16[1,256,2048]{2,1,0:T(8,128)(2,1)} %param.16) | copy-start | bytes 3145732
  7.2 11.0 copy-start.8
  9.6 25.5 %all-to-all-start = ((bf16[256,32,1,64]{0,3,2,1:T(8,128)(2,1)}), bf16[256,32,1,64]{0,3,2,1:T(8,128)(2,1)S(1)}, u32[]{:S(2)}, u32[]{:S(2)}) async-start(bf16[256,32,1,64]{0,3,2,1:T(8,128)(2,1)} %bitcast.1), calls=%async_computation | async-start | bytes 2097152 | tf_op jit(solution)/shard_map/all_to_all | solution.py:150
  35.1 20.9 %all-to-all-start.1 = ((bf16[256,32,1,64]{0,3,2,1:T(8,128)(2,1)}), bf16[256,32,1,64]{0,3,2,1:T(8,128)(2,1)S(1)}, u32[]{:S(2)}, u32[]{:S(2)}) async-start(bf16[256,32,1,64]{0,3,2,1:T(8,128)(2,1)} %bitcast.288), calls=%async_computation.1 | async-start | bytes 2097152 | tf_op jit(solution)/shard_map/all_to_all | solution.py:149
  56.0 5.4 copy-start.9
  56.0 5.4 copy-start.10
  56.0 21.6 %all-to-all-start.2 = ((bf16[256,32,1,64]{0,3,2,1:T(8,128)(2,1)}), bf16[256,32,1,64]{0,3,2,1:T(8,128)(2,1)}, u32[]{:S(2)}, u32[]{:S(2)}) async-start(bf16[256,32,1,64]{0,3,2,1:T(8,128)(2,1)} %bitcast.10), calls=%async_computation.2 | async-start | bytes 2097152 | tf_op jit(solution)/shard_map/all_to_all | solution.py:151
  60.6 145.3 %all-gather.3.cloned.1.call-start = ((), (), s32[]{:S(2)}) async-start(), calls=%async_computation.9 | async-start | bytes 10485760 | tf_op jit(solution)/shard_map/all_gather | solution.py:134
  214.9 118.7 %all-to-all-start.3 = ((bf16[256,32,1,64]{0,3,2,1:T(8,128)(2,1)}), bf16[256,32,1,64]{0,3,2,1:T(8,128)(2,1)}, u32[]{:S(2)}, u32[]{:S(2)}) async-start(bf16[256,32,1,64]{0,3,2,1:T(8,128)(2,1)} %bitcast.285), calls=%async_computation.3 | async-start | bytes 2097152 | tf_op jit(solution)/shard_map/all_to_all | solution.py:152
  219.3 847.2 %reduce-scatter.2.cloned.1.call-start = ((), (), s32[]{:S(2)}) async-start(), calls=%async_computation.10 | async-start | bytes 16908288 | tf_op jit(solution)/shard_map/reduce_scatter | solution.py:164
  409.8 1.2 copy-start.7
  409.8 1399.3 %all-gather.5.cloned.1.call-start = ((), (), s32[]{:S(2)}) async-start(), calls=%async_computation.11 | async-start | bytes 2162688 | tf_op jit(solution)/shard_map/all_gather | solution.py:172
  1085.9 3.8 copy-start.2
  1085.9 3.8 copy-start.3
  1092.6 10.4 copy-start.4
  1133.2 4.4 copy-start.2
  1133.2 4.4 copy-start.3
  1140.5 10.4 copy-start.4
  1181.0 4.4 copy-start.2
  1181.0 4.4 copy-start.3
  1188.3 10.3 copy-start.4
  1228.7 4.4 copy-start.2
  1228.7 4.4 copy-start.3
  1236.0 10.3 copy-start.4
  1276.4 4.4 copy-start.2
  1276.4 4.4 copy-start.3
  1283.7 10.3 copy-start.4
  1324.2 4.4 copy-start.2
  1324.2 4.4 copy-start.3
  1331.5 10.3 copy-start.4
  1371.9 4.4 copy-start.2
  1371.9 4.4 copy-start.3
  1379.2 10.4 copy-start.4
  1419.7 4.4 copy-start.2
  1419.7 4.4 copy-start.3
  1427.0 10.3 copy-start.4
  1467.4 4.4 copy-start.2
  1467.4 4.4 copy-start.3
  1474.7 10.3 copy-start.4
  1515.2 4.4 copy-start.2
  1515.2 4.4 copy-start.3
  1522.5 10.3 copy-start.4
  1603.9 17.3 copy-start.5
  1608.7 71.1 %all-to-all-start.4 = ((bf16[32,2,8192]{2,1,0:T(2,128)(2,1)}), bf16[32,2,8192]{2,1,0:T(2,128)(2,1)}, u32[]{:S(2)}, u32[]{:S(2)}) async-start(bf16[32,2,8192]{2,1,0:T(2,128)(2,1)} %reshape.269), calls=%async_computation.4 | async-start | bytes 2097152 | tf_op jit(solution)/shard_map/all_to_all | solution.py:158
  1675.1 12.8 copy-start.6
  1679.8 62.8 %all-to-all-start.5 = ((bf16[32,2,8192]{2,1,0:T(2,128)(2,1)}), bf16[32,2,8192]{2,1,0:T(2,128)(2,1)}, u32[]{:S(2)}, u32[]{:S(2)}) async-start(bf16[32,2,8192]{2,1,0:T(2,128)(2,1)} %reshape.271), calls=%async_computation.5 | async-start | bytes 2097152 | tf_op jit(solution)/shard_map/all_to_all | solution.py:159
  1742.7 49.0 %all-to-all-start.6 = ((bf16[32,2,8192]{2,1,0:T(2,128)(2,1)}), bf16[32,2,8192]{2,1,0:T(2,128)(2,1)S(1)}, u32[]{:S(2)}, u32[]{:S(2)}) async-start(bf16[32,2,8192]{2,1,0:T(2,128)(2,1)} %reshape.273), calls=%async_computation.6 | async-start | bytes 2097152 | tf_op jit(solution)/shard_map/all_to_all | solution.py:160
  1807.7 5.6 copy-start.1
Sparse Core Ops, SparseCore 0:
  63.1 85.3 all-gather.2
  409.9 656.5 reduce-scatter.1
  1068.8 44.7 all-gather.4
where the time goes:
time: 1840 us; the launch traced here: 1820 us
  waiting for transfers between devices  693 us (38%)
  other arithmetic  394 us (21%)
  matrix products  337 us (18%)
  local copies, waits for them, and re-layouts  246 us (13%)
  loops' own time  59.4 us (3%)
  starting transfers between devices  50.5 us (3%)
  blocking collectives  24.5 us (1%)
    reduce_scatter x1, waiting for transfers between devices, on_device(): lax.psum_scatter(lax.dot_general(attn_out, loss_grad, (((0,), (0,)), ((),...  654 us
    reshape x3, other arithmetic, head_backward(): accum.astype(jnp.bfloat16).reshape(-1, head_count, HD)  138 us
    scatter-add x10, other arithmetic, grad_step(): value_accum = value_accum.at[picked].add(value_terms)  103 us
    scatter-add x10, other arithmetic, grad_step(): key_accum = key_accum.at[picked].add(key_terms)  103 us
    dot_general x20, matrix products, pair_scores(): jnp.einsum('iqhd,ikhd->ihqk', query_blocks, chosen, preferred_element_typ...  93.1 us
    unnamed x41, local copies, waits for them, and re-layouts  77.5 us
    dot_general x10, matrix products, output_step(): jnp.einsum('ihqk,ikhd->iqhd', prob_half, value_heads[picked], preferred_e...  55.2 us
    dot_general x10, matrix products, grad_step(): jnp.einsum('iqhd,ikhd->ihqk', grad_blocks, chosen_values, preferred_eleme...  51 us
  transfers between devices with their start and end apart: 10, of which 4 were waited for; matrix products, arithmetic and copies ran while one was open for 50% of the time, Pallas kernels for 0%

commit v1 on v0

v1 whole, which is shorter than its diff:
```python
import jax
import jax.numpy as jnp
from jax import lax
from jax.experimental import pallas as pl
from jax.experimental.pallas import tpu as pltpu
from jax.sharding import PartitionSpec as P

HEADS = 32
HD = 64
BLK = 128
MAXK = 10
LOG2E = 1.4426950408889634


def attention_kernel(adj_ref, count_ref, qg_ref, kv_ref, dqo_ref, dkv_ref, acc_ref, kvt_ref, sd_ref, te_ref):
    blocks = qg_ref.shape[0] // BLK
    lane = lax.broadcasted_iota(jnp.int32, (BLK, BLK), 1)
    first = lane < HD
    half_scale = jnp.where(first, HD ** -0.5, 1.0).astype(jnp.float32)
    score_scale = HD ** -0.5 * LOG2E

    def rows(b):
        return pl.ds(pl.multiple_of(b * BLK, BLK), BLK)

    @pl.loop(0, blocks)
    def _(b):
        acc_ref[rows(b), :] = jnp.zeros((BLK, BLK), jnp.float32)
        kvt_ref[rows(b), :] = kv_ref[rows(b), :].T

    def fold(x, op):
        parts = [x[r * 8:(r + 1) * 8] for r in range(x.shape[0] // 8)]
        while len(parts) > 1:
            parts = [op(parts[t], parts[t + 1]) for t in range(0, len(parts) - 1, 2)] + (
                [parts[-1]] if len(parts) % 2 else [])
        return parts[0]

    def one_block(i, n):
        qg = qg_ref[rows(i), :]
        zero = jnp.zeros_like(qg)
        pair = jnp.concatenate([jnp.where(first, qg, zero), jnp.where(first, zero, qg)], axis=0)
        picked = [adj_ref[i, j] for j in range(n)]
        top = None
        for j in range(n):
            sd = lax.dot_general(
                kv_ref[rows(picked[j]), :], pair, (((1,), (1,)), ((), ())),
                preferred_element_type=jnp.float32)
            sd_ref[j * BLK:(j + 1) * BLK, :] = sd
            part = fold(sd[:, :BLK], jnp.maximum)
            top = part if top is None else jnp.maximum(top, part)
        top = jnp.max(top, axis=0, keepdims=True) * score_scale
        total = None
        dots = None
        for j in range(n):
            at = slice(j * BLK, (j + 1) * BLK)
            expo = jnp.exp2(sd_ref[at, :BLK] * score_scale - top)
            sd_ref[at, :BLK] = expo
            part = fold(expo, jnp.add)
            total = part if total is None else total + part
            part = fold(expo * sd_ref[at, BLK:], jnp.add)
            dots = part if dots is None else dots + part
        inv = 1.0 / jnp.sum(total, axis=0, keepdims=True)
        row_dot = jnp.sum(dots, axis=0, keepdims=True) * inv
        out = None
        for j in range(n):
            at = slice(j * BLK, (j + 1) * BLK)
            prob = sd_ref[at, :BLK] * inv
            grad = prob * (sd_ref[at, BLK:] - row_dot)
            te = jnp.concatenate([grad.astype(jnp.bfloat16), prob.astype(jnp.bfloat16)], axis=1)
            te_ref[at, :] = te
            acc_ref[rows(picked[j]), :] += jnp.dot(te, pair, preferred_element_type=jnp.float32)
        kvt = jnp.concatenate([kvt_ref[rows(picked[j]), :] for j in range(n)], axis=1)
        out = jnp.dot(kvt, te_ref[:n * BLK, :], preferred_element_type=jnp.float32)
        both = jnp.concatenate([out[:HD, :BLK], out[HD:, BLK:]], axis=0).T
        dqo_ref[rows(i), :] = (both * half_scale).astype(jnp.bfloat16)

    @pl.loop(0, blocks)
    def _(i):
        count = count_ref[i]
        for n in range(2, MAXK + 1):
            @pl.when(count == n)
            def _():
                one_block(i, n)

    @pl.loop(0, blocks)
    def _(b):
        dkv_ref[rows(b), :] = (acc_ref[rows(b), :] * half_scale).astype(jnp.bfloat16)


def attention(adjacency, counts, qg, kv):
    tokens = qg.shape[0]
    whole = pl.BlockSpec(memory_space=pltpu.VMEM)
    scalar = pl.BlockSpec(memory_space=pltpu.SMEM)
    shape = jax.ShapeDtypeStruct((tokens, 2 * HD), jnp.bfloat16)
    return pl.pallas_call(
        attention_kernel,
        out_shape=(shape, shape),
        in_specs=[scalar, scalar, whole, whole],
        out_specs=(whole, whole),
        scratch_shapes=[
            pltpu.VMEM((tokens, 2 * HD), jnp.float32),
            pltpu.VMEM((tokens, 2 * HD), jnp.bfloat16),
            pltpu.VMEM((MAXK * BLK, 2 * BLK), jnp.float32),
            pltpu.VMEM((MAXK * BLK, 2 * BLK), jnp.bfloat16),
        ],
        compiler_params=pltpu.CompilerParams(vmem_limit_bytes=48 << 20),
    )(adjacency, counts, qg, kv)


def pack_kernel(left_ref, right_ref, out_ref):
    for j in range(HEADS // 2):
        at = slice(j * 2 * HD, (j + 1) * 2 * HD)
        left, right = left_ref[:, at], right_ref[:, at]
        out_ref[2 * j] = jnp.concatenate([left[:, :HD], right[:, :HD]], axis=1)
        out_ref[2 * j + 1] = jnp.concatenate([left[:, HD:], right[:, HD:]], axis=1)


def pack(left, right):
    whole = pl.BlockSpec(memory_space=pltpu.VMEM)
    return pl.pallas_call(
        pack_kernel,
        out_shape=jax.ShapeDtypeStruct((HEADS, left.shape[0], 2 * HD), left.dtype),
        in_specs=[whole, whole],
        out_specs=whole,
    )(left, right)


def unpack_kernel(in_ref, left_ref, right_ref):
    for j in range(HEADS // 2):
        at = slice(j * 2 * HD, (j + 1) * 2 * HD)
        one, two = in_ref[2 * j], in_ref[2 * j + 1]
        left_ref[:, at] = jnp.concatenate([one[:, :HD], two[:, :HD]], axis=1)
        right_ref[:, at] = jnp.concatenate([one[:, HD:], two[:, HD:]], axis=1)


def unpack(packed):
    whole = pl.BlockSpec(memory_space=pltpu.VMEM)
    shape = jax.ShapeDtypeStruct((packed.shape[1], HEADS * HD), packed.dtype)
    return pl.pallas_call(
        unpack_kernel,
        out_shape=(shape, shape),
        in_specs=[whole],
        out_specs=(whole, whole),
    )(packed)


def exchange(packed):
    return lax.all_to_all(packed, "seq", split_axis=0, concat_axis=0, tiled=True)


def on_device(queries, keys, values, out_grad, out_weight, key_blocks, block_counts):
    local_tokens, width = queries.shape[1:]
    parts = lax.axis_size("seq")
    loss_grad = out_grad[0]
    kv = exchange(pack(keys[0], values[0])).reshape(-1, 2 * HD)
    attn_grad = lax.dot_general(
        loss_grad,
        lax.all_gather(out_weight, "fsdp", axis=0, tiled=True),
        (((1,), (1,)), ((), ())),
        preferred_element_type=jnp.float32,
    ).astype(jnp.bfloat16)
    qg = exchange(pack(queries[0], attn_grad)).reshape(-1, 2 * HD)
    dqo, dkv = attention(key_blocks[0], block_counts[0], qg, kv)
    query_grad, attn_out = unpack(exchange(dqo.reshape(parts, local_tokens, 2 * HD)))
    term = lax.dot_general(
        attn_out, loss_grad, (((0,), (0,)), ((), ())), preferred_element_type=jnp.float32
    ).astype(jnp.bfloat16)
    planes = lax.axis_size("fsdp")
    term = term.reshape(planes, parts, width // planes // parts, width).transpose(1, 0, 2, 3)
    term = lax.all_to_all(term, "seq", split_axis=0, concat_axis=0, tiled=True)
    term = jnp.sum(term.astype(jnp.float32), axis=0).astype(jnp.bfloat16)
    term = lax.all_to_all(term, "fsdp", split_axis=0, concat_axis=0, tiled=True)
    share = jnp.sum(term.astype(jnp.float32), axis=0)
    wo_grad = lax.all_gather(share.astype(jnp.bfloat16), "seq", axis=0, tiled=True).astype(jnp.float32)
    key_grad, value_grad = unpack(exchange(dkv.reshape(parts, local_tokens, 2 * HD)))
    return (query_grad[None], key_grad[None], value_grad[None], wo_grad)


def solution(mesh):
    return jax.shard_map(
        on_device,
        mesh=mesh,
        in_specs=(
            P("fsdp", "seq", None),
            P("fsdp", "seq", None),
            P("fsdp", "seq", None),
            P("fsdp", "seq", None),
            P("fsdp", None),
            P("fsdp", None, None),
            P("fsdp", None),
        ),
        out_specs=(
            P("fsdp", "seq", None),
            P("fsdp", "seq", None),
            P("fsdp", "seq", None),
            P("fsdp", None),
        ),
        check_vma=False,
    )
```

time: 1840 us -> 436 us (0.24); the launches traced: 1820 us -> 436 us
  waiting for transfers between devices: 693 us -> 116 us
  other arithmetic: 394 us -> 10.3 us
  matrix products: 337 us -> 13.6 us
  local copies, waits for them, and re-layouts: 246 us -> 9.68 us
  blocking collectives: 24.5 us -> 175 us
  Pallas kernels: 0 us -> 80.2 us
  loops' own time: 59.4 us -> 0 us
  starting transfers between devices: 50.5 us -> 16.3 us
    reduce_scatter x1 -> x0, waiting for transfers between devices: 654 us -> none  [on_device(): lax.psum_scatter(lax.dot_general(attn_out, loss_grad, (((0,), (0,)), ((),...]
    dot_general x70 -> x0, matrix products: 322 us -> none  [the longest x20 93.1 us: pair_scores(): jnp.einsum('iqhd,ikhd->ihqk', query_blocks, chosen, preferred_element_typ...]
    scatter-add x20 -> x0, other arithmetic: 207 us -> none  [the longest x10 103 us: grad_step(): value_accum = value_accum.at[picked].add(value_terms)]
    all_to_all x1 -> x4, blocking collectives: 24.5 us -> 175 us  [the longest x1 100 us: on_device(): term = lax.all_to_all(term, 'seq', split_axis=0, concat_axis=0, tiled=True)]
    reshape x4 -> x0, other arithmetic: 141 us -> none  [the longest x3 138 us: head_backward(): accum.astype(jnp.bfloat16).reshape(-1, head_count, HD)]
    pallas_call x0 -> x5, Pallas kernels: none -> 80.2 us  [the longest x1 65.9 us: attention(): pl.pallas_call(attention_kernel, out_shape=(shape, shape), in_specs=[scal...]
    all_gather x1, waiting for transfers between devices: 0.02 us -> 76.2 us  [on_device(): lax.all_gather(out_weight, 'fsdp', axis=0, tiled=True)]
    unnamed x41 -> x11, local copies, waits for them, and re-layouts: 77.5 us -> 1.42 us
  transfers between devices with their start and end apart: 10 -> 4, of which waited for: 4 -> 3; matrix products, arithmetic and copies ran while one was open for 50% -> 2% of each run, Pallas kernels for 0% -> 2%
where the time goes in v1:
time: 436 us
  blocking collectives  175 us (40%)
  waiting for transfers between devices  116 us (27%)
  Pallas kernels  80.2 us (18%)
  starting transfers between devices  16.3 us (4%)
  between operations  14.1 us (3%)
  matrix products  13.6 us (3%)
  other arithmetic  10.3 us (2%)
  local copies, waits for them, and re-layouts  9.68 us (2%)
    all_to_all x1, blocking collectives, on_device(): term = lax.all_to_all(term, 'seq', split_axis=0, concat_axis=0, tiled=True)  100 us
    all_gather x1, waiting for transfers between devices, on_device(): lax.all_gather(out_weight, 'fsdp', axis=0, tiled=True)  76.2 us
    all_to_all x2, blocking collectives, exchange(): lax.all_to_all(packed, 'seq', split_axis=0, concat_axis=0, tiled=True)  66.3 us
    pallas_call x1, Pallas kernels, attention(): pl.pallas_call(attention_kernel, out_shape=(shape, shape), in_specs=[scal...  65.9 us
    all_to_all x2, waiting for transfers between devices, exchange(): lax.all_to_all(packed, 'seq', split_axis=0, concat_axis=0, tiled=True)  28.2 us
    all_to_all x2, starting transfers between devices, exchange(): lax.all_to_all(packed, 'seq', split_axis=0, concat_axis=0, tiled=True)  16.2 us
    all_gather x1, waiting for transfers between devices, on_device(): lax.all_gather(share.astype(jnp.bfloat16), 'seq', axis=0, tiled=True)  10.9 us
    all_to_all x1, blocking collectives, on_device(): term = lax.all_to_all(term, 'fsdp', split_axis=0, concat_axis=0, tiled=True)  8.77 us
  transfers between devices with their start and end apart: 4, of which 3 were waited for; matrix products, arithmetic and copies ran while one was open for 2% of the time, Pallas kernels for 2%

profile of v1, /device:TPU:1, one launch (start us, length us, event | category | flops | bytes accessed | tf_op | source)
XLA Modules:
  0.0 435.6 jit_solution(4635085137148034600)
XLA Ops:
  7.2 0.0 copy-start
  7.2 0.0 all-gather.3.cloned.1.call-start
  7.2 0.7 all-gather.3.cloned.1.call-update
  7.9 3.5 shard_map.103
  11.4 8.6 %all-to-all-start.1 = ((bf16[32,256,128]{2,1,0:T(8,128)(2,1)}), bf16[32,256,128]{2,1,0:T(8,128)(2,1)S(1)}, u32[]{:S(2)}, u32[]{:S(2)}) async-start(bf16[32,256,128]{2,1,0:T(8,128)(2,1)} %shard_map.103), calls=%async_computation.1 | async-start | bytes 4194304 | tf_op jit(solution)/shard_map/all_to_all | solution.py:147
  20.0 76.2 %all-gather.3.cloned.1.call-done = bf16[2048,2048]{1,0:T(8,128)(2,1)} async-done(((bf16[512,2048]{1,0:T(8,128)(2,1)}), bf16[2048,2048]{1,0:T(8,128)(2,1)}) %all-gather.3.cloned.1.call-update) | async-done | bytes 8388624 | tf_op jit(solution)/shard_map/all_gather | solution.py:157
  96.2 0.0 copy-done
  96.2 6.7 %convolution_convert_fusion.1.right_ref = bf16[256,2048]{1,0:T(8,128)(2,1)} fusion(bf16[2048,2048]{1,0:T(8,128)(2,1)} %all-gather.3.cloned.1.call-done, bf16[1,256,2048]{2,1,0:T(8,128)(2,1)S(1)} %copy-done), kind=kOutput, calls=%fused_computation.2 | convolution fusion | flops 2148007936 | bytes 10485760 | tf_op jit(solution)/shard_map/dot_general | solution.py:155
  103.0 3.5 shard_map.102
  106.4 0.0 copy-start.4
  106.4 0.0 copy-start.2
  106.4 0.0 all-to-all-done.1
  106.4 0.0 copy-start.3
  106.5 1.3 copy-done.3
  107.8 7.6 %all-to-all-start = ((bf16[32,256,128]{2,1,0:T(8,128)(2,1)}), bf16[32,256,128]{2,1,0:T(8,128)(2,1)}, u32[]{:S(2)}, u32[]{:S(2)}) async-start(bf16[32,256,128]{2,1,0:T(8,128)(2,1)} %shard_map.102), calls=%async_computation | async-start | bytes 4194304 | tf_op jit(solution)/shard_map/all_to_all | solution.py:147
  115.4 0.0 all-gather.5.cloned.1.call-start
  115.4 0.0 copy-done.4
  115.5 0.1 copy.14
  115.6 28.2 %all-to-all-done = bf16[32,256,128]{2,1,0:T(8,128)(2,1)} async-done(((bf16[32,256,128]{2,1,0:T(8,128)(2,1)}), bf16[32,256,128]{2,1,0:T(8,128)(2,1)}, u32[]{:S(2)}, u32[]{:S(2)}) %all-to-all-start) | async-done | bytes 2097184 | tf_op jit(solution)/shard_map/all_to_all | solution.py:147
  143.7 0.0 copy-done.2
  143.7 65.9 %shard_map.104 = (bf16[8192,128]{1,0:T(8,128)(2,1)S(1)}, bf16[8192,128]{1,0:T(8,128)(2,1)S(1)}) custom-call(s32[64,10]{1,0:T(8,128)S(1)} %bitcast.25, s32[64]{0:T(128)S(1)} %bitcast.26, bf16[8192,128]{1,0:T(8,128)(2,1)} %bitcast.4.qg_ref, bf16[8192,128]{1,0:T(8,128)(2,1)} %bitcast.29), custom_call_target="tpu_custom_call" | custom-call | tf_op jit(solution)/shard_map/pallas_call | solution.py:94
  209.7 32.4 %all_to_all.30.in_ref = bf16[32,256,128]{2,1,0:T(8,128)(2,1)} all-to-all(bf16[32,256,128]{2,1,0:T(8,128)(2,1)S(1)} %bitcast.24), channel_id=1, replica_groups=mesh['fsdp'=4,'seq'=32] {'seq'}, dimensions={0} | all-to-all | bytes 4194304 | tf_op jit(solution)/shard_map/all_to_all | solution.py:147
  242.1 3.6 shard_map.105
  245.7 6.8 %convolution_convert_fusion = bf16[2048,2048]{1,0:T(8,128)(2,1)} fusion(bf16[256,2048]{1,0:T(8,128)(2,1)} %get-tuple-element.15, bf16[1,256,2048]{2,1,0:T(8,128)(2,1)S(1)} %copy-done), kind=kOutput, calls=%fused_computation.1 | convolution fusion | flops 2151677952 | bytes 10485760 | tf_op jit(solution)/shard_map/dot_general | solution.py:164
  252.6 8.3 %copy.17 = bf16[4,32,16,2048]{3,2,0,1:T(8,128)(2,1)} copy(bf16[4,32,16,2048]{3,2,1,0:T(8,128)(2,1)} %bitcast.27) | data formatting | bytes 16777216 | tf_op jit(solution)/shard_map/reshape | solution.py:168
  260.8 100.4 %all_to_all.31 = bf16[32,4,16,2048]{3,2,1,0:T(8,128)(2,1)} all-to-all(bf16[32,4,16,2048]{3,2,1,0:T(8,128)(2,1)} %bitcast.28), channel_id=1, replica_groups=mesh['fsdp'=4,'seq'=32] {'seq'}, dimensions={0} | all-to-all | bytes 16777216 | tf_op jit(solution)/shard_map/all_to_all | solution.py:169
  361.2 5.5 %reduce_sum.24 = bf16[4,16,2048]{2,1,0:T(8,128)(2,1)S(1)} reduce(bf16[32,4,16,2048]{3,2,1,0:T(8,128)(2,1)} %all_to_all.31, bf16[]{:T(256)} %constant.3.clone.1), dimensions={0}, to_apply=%region_0.0 | reduce | flops 4063232 | bytes 8650754 | tf_op jit(solution)/shard_map/reduce_sum | solution.py:170
  366.7 8.8 %all_to_all.32 = bf16[4,16,2048]{2,1,0:T(8,128)(2,1)S(1)} all-to-all(bf16[4,16,2048]{2,1,0:T(8,128)(2,1)S(1)} %reduce_sum.24), channel_id=1, replica_groups=mesh['fsdp'=4,'seq'=32] {'fsdp'}, dimensions={0} | all-to-all | bytes 524288 | tf_op jit(solution)/shard_map/all_to_all | solution.py:171
  375.5 0.7 reduce_sum.25
  376.2 0.0 all-gather.5.cloned.1.call-update
  376.2 33.9 %all_to_all.33.in_ref = bf16[32,256,128]{2,1,0:T(8,128)(2,1)} all-to-all(bf16[32,256,128]{2,1,0:T(8,128)(2,1)S(1)} %bitcast.23), channel_id=1, replica_groups=mesh['fsdp'=4,'seq'=32] {'seq'}, dimensions={0} | all-to-all | bytes 4194304 | tf_op jit(solution)/shard_map/all_to_all | solution.py:147
  410.1 0.0 copy-start.1
  410.1 3.7 shard_map.106
  413.8 10.9 %all-gather.5.cloned.1.call-done = bf16[512,2048]{1,0:T(8,128)(2,1)} async-done(((bf16[16,2048]{1,0:T(8,128)(2,1)}), bf16[512,2048]{1,0:T(8,128)(2,1)}) %all-gather.5.cloned.1.call-update) | async-done | bytes 2097168 | tf_op jit(solution)/shard_map/all_gather | solution.py:173
  424.6 4.1 convert_element_type.15
  428.8 0.0 copy-done.1
Async XLA Ops:
  7.2 89.1 %copy-start = (bf16[1,256,2048]{2,1,0:T(8,128)(2,1)S(1)}, bf16[1,256,2048]{2,1,0:T(8,128)(2,1)}, u32[]{:S(2)}) copy-start(bf16[1,256,2048]{2,1,0:T(8,128)(2,1)} %param.10) | copy-start | bytes 3145732
  7.2 89.1 %all-gather.3.cloned.1.call-start = ((), (), s32[]{:S(2)}) async-start(), calls=%async_computation.6 | async-start | bytes 10485760 | tf_op jit(solution)/shard_map/all_gather | solution.py:157
  11.4 95.0 %all-to-all-start.1 = ((bf16[32,256,128]{2,1,0:T(8,128)(2,1)}), bf16[32,256,128]{2,1,0:T(8,128)(2,1)S(1)}, u32[]{:S(2)}, u32[]{:S(2)}) async-start(bf16[32,256,128]{2,1,0:T(8,128)(2,1)} %shard_map.103), calls=%async_computation.1 | async-start | bytes 4194304 | tf_op jit(solution)/shard_map/all_to_all | solution.py:147
  106.4 9.0 %copy-start.4 = (s32[1,64,10]{1,0,2:T(1,128)S(1)}, s32[1,64,10]{1,0,2:T(1,128)}, u32[]{:S(2)}) copy-start(s32[1,64,10]{1,0,2:T(1,128)} %param.12) | copy-start | bytes 7684
  106.4 37.3 %copy-start.2 = (s32[1,64]{1,0:T(1,128)S(1)}, s32[1,64]{1,0:T(1,128)}, u32[]{:S(2)}) copy-start(s32[1,64]{1,0:T(1,128)} %param.13) | copy-start | bytes 772
  106.4 1.3 copy-start.3
  107.8 36.0 %all-to-all-start = ((bf16[32,256,128]{2,1,0:T(8,128)(2,1)}), bf16[32,256,128]{2,1,0:T(8,128)(2,1)}, u32[]{:S(2)}, u32[]{:S(2)}) async-start(bf16[32,256,128]{2,1,0:T(8,128)(2,1)} %shard_map.102), calls=%async_computation | async-start | bytes 4194304 | tf_op jit(solution)/shard_map/all_to_all | solution.py:147
  115.4 309.2 %all-gather.5.cloned.1.call-start = ((), (), s32[]{:S(2)}) async-start(), calls=%async_computation.7 | async-start | bytes 2162688 | tf_op jit(solution)/shard_map/all_gather | solution.py:173
  410.1 18.7 %copy-start.1 = (bf16[1,256,2048]{2,1,0:T(8,128)(2,1)S(1)}, bf16[1,256,2048]{2,1,0:T(8,128)(2,1)}, u32[]{:S(2)}) copy-start(bf16[1,256,2048]{2,1,0:T(8,128)(2,1)} %param.10) | copy-start | bytes 3145732
Sparse Core Ops, SparseCore 0:
  9.7 86.5 all-gather.2
  376.3 48.2 all-gather.4

commit v2 on v1

v2 whole, which is shorter than its diff:
```python
import jax
import jax.numpy as jnp
from jax import lax
from jax.experimental import pallas as pl
from jax.experimental.pallas import tpu as pltpu
from jax.sharding import PartitionSpec as P

HEADS = 32
HD = 64
BLK = 128
MAXK = 10
LOG2E = 1.4426950408889634
SEQ = 32
SIDE = 4
CHIPS = 16
PLANES = 4
D = 2048
ROWS = 256
BF = jnp.bfloat16
F32 = jnp.float32
PARTS = ((0, 768), (768, 640), (1408, 640))


def remote(src, dst, send_sem, recv_sem, **where):
    return pltpu.make_async_remote_copy(
        src_ref=src, dst_ref=dst, send_sem=send_sem, recv_sem=recv_sem,
        device_id=where, device_id_type=pl.DeviceIdType.MESH)


def local(src, dst, sem):
    return pltpu.make_async_copy(src, dst, sem)


def position():
    plane, member = lax.axis_index("fsdp"), lax.axis_index("seq")
    chip, core = lax.div(member, 2), lax.rem(member, 2)
    return plane, member, chip, core, lax.div(chip, SIDE), lax.rem(chip, SIDE)


def entry_barrier(plane, member):
    barrier = pltpu.get_barrier_semaphore()

    @pl.loop(1, SEQ)
    def _(k):
        pl.semaphore_signal(
            barrier, inc=1, device_id={"seq": lax.rem(member + k, SEQ)},
            device_id_type=pl.DeviceIdType.MESH)

    @pl.loop(1, PLANES)
    def _(k):
        pl.semaphore_signal(
            barrier, inc=1, device_id={"fsdp": lax.rem(plane + k, PLANES)},
            device_id_type=pl.DeviceIdType.MESH)

    pl.semaphore_wait(barrier, SEQ + PLANES - 2)


def halves(one, two):
    return (jnp.concatenate([one[:, :HD], two[:, :HD]], axis=1),
            jnp.concatenate([one[:, HD:], two[:, HD:]], axis=1))


def head_kernel(q_ref, k_ref, v_ref, og_ref, w_ref, q_out, kv_out, g_out, both_out,
                q_pack, kv_pack, g_pack, both_ref, w_buf,
                q_send, kv_send, g_send, q_recv, kv_recv, g_recv,
                w_send, w_recv, w_own, both_send, both_recv, both_own):
    plane, member, chip, core, _, _ = position()
    up, down = lax.rem(plane + 1, PLANES), lax.rem(plane + 3, PLANES)
    far = lax.rem(plane + 2, PLANES)
    sibling = chip * 2 + 1 - core
    mine = pl.ds(pl.multiple_of(core * ROWS, ROWS), ROWS)
    w_mine = local(w_ref.at[mine], w_buf.at[plane], w_own.at[0])
    w_mine.start()
    both_mine = local(og_ref, both_ref.at[mine], w_own.at[1])
    both_mine.start()
    entry_barrier(plane, member)
    w_up = remote(w_ref.at[mine], w_buf.at[plane], w_send.at[0], w_recv.at[0], fsdp=up)
    w_down = remote(w_ref.at[mine], w_buf.at[plane], w_send.at[1], w_recv.at[1], fsdp=down)
    w_up.start()
    w_down.start()
    both_copy = remote(og_ref, both_ref.at[mine], both_send, both_recv, seq=sibling)
    both_copy.start()

    def send(block, head, out, slot, send_sem, recv_sem):
        @pl.when(head != member)
        def _():
            remote(block, out.at[slot], send_sem, recv_sem, seq=head).start()

        @pl.when(head == member)
        def _():
            local(block, out.at[slot], recv_sem).start()

    def sent(block, head, out, slot, send_sem, recv_sem):
        @pl.when(head != member)
        def _():
            remote(block, out.at[slot], send_sem, recv_sem, seq=head).wait_send()

    @pl.loop(0, CHIPS)
    def _(k):
        j = lax.rem(chip + k, CHIPS)
        at = pl.ds(pl.multiple_of(j * 2 * HD, 2 * HD), 2 * HD)
        kv = halves(k_ref[:, at], v_ref[:, at])
        for e in range(2):
            kv_pack[2 * j + e] = kv[e]
            send(kv_pack.at[2 * j + e], 2 * j + e, kv_out, member, kv_send.at[2 * j + e], kv_recv)

    @pl.loop(0, CHIPS)
    def _(k):
        j = lax.rem(chip + k, CHIPS)
        at = pl.ds(pl.multiple_of(j * 2 * HD, 2 * HD), 2 * HD)
        q = halves(q_ref[:BLK, at], q_ref[BLK:, at])
        for e in range(2):
            q_pack[2 * j + e] = q[e]
            send(q_pack.at[2 * j + e], 2 * j + e, q_out, member, q_send.at[2 * j + e], q_recv)

    def project(which):
        for pair in range(2):
            grad = lax.dot_general(
                both_ref[...], w_buf[which, pair * BLK:(pair + 1) * BLK, :],
                (((1,), (1,)), ((), ())), preferred_element_type=F32).astype(BF)
            top = halves(grad[:BLK], grad[BLK:2 * BLK])
            low = halves(grad[2 * BLK:3 * BLK], grad[3 * BLK:])
            for e in range(2):
                slot = which * SIDE + pair * 2 + e
                head = which * 2 * SIDE + core * SIDE + pair * 2 + e
                g_pack[slot, :BLK, :] = top[e]
                g_pack[slot, BLK:, :] = low[e]
                send(g_pack.at[slot], head, g_out, chip, g_send.at[slot], g_recv)

    w_mine.wait()
    both_mine.wait()
    both_copy.wait()
    both_write = local(both_ref, both_out, both_own)
    both_write.start()
    project(plane)
    w_up.wait()
    first = pl.ds(0, BLK)
    second = pl.ds(BLK, BLK)
    pass_up = remote(w_buf.at[down, first], w_buf.at[down, first], w_send.at[2], w_recv.at[2], fsdp=up)
    pass_up.start()
    w_down.wait()
    pass_down = remote(w_buf.at[up, second], w_buf.at[up, second], w_send.at[3], w_recv.at[3], fsdp=down)
    pass_down.start()
    project(down)
    project(up)
    pass_up.wait()
    pass_down.wait()
    project(far)
    both_write.wait()

    @pl.loop(0, SEQ)
    def _(d):
        sent(kv_pack.at[d], d, kv_out, member, kv_send.at[d], kv_recv)
        sent(q_pack.at[d], d, q_out, member, q_send.at[d], q_recv)

    @pl.loop(0, CHIPS)
    def _(slot):
        head = lax.div(slot, SIDE) * 2 * SIDE + core * SIDE + lax.rem(slot, SIDE)
        sent(g_pack.at[slot], head, g_out, chip, g_send.at[slot], g_recv)

    local(kv_out, kv_out, kv_recv).wait()
    local(q_out, q_out, q_recv).wait()
    local(g_out, g_out, g_recv).wait()


def head_exchange(queries, keys, values, out_grad, out_weight):
    anyway = pl.BlockSpec(memory_space=pl.ANY)
    whole = pl.BlockSpec(memory_space=pltpu.VMEM)
    dma = pltpu.SemaphoreType.DMA
    return pl.pallas_call(
        head_kernel,
        out_shape=(
            jax.ShapeDtypeStruct((SEQ, BLK, 2 * HD), BF),
            jax.ShapeDtypeStruct((SEQ, ROWS, 2 * HD), BF),
            jax.ShapeDtypeStruct((CHIPS, ROWS, 2 * HD), BF),
            jax.ShapeDtypeStruct((2 * ROWS, D), BF),
        ),
        in_specs=[whole, whole, whole, whole, anyway],
        out_specs=(anyway, anyway, anyway, anyway),
        scratch_shapes=[
            pltpu.VMEM((SEQ, BLK, 2 * HD), BF),
            pltpu.VMEM((SEQ, ROWS, 2 * HD), BF),
            pltpu.VMEM((CHIPS, ROWS, 2 * HD), BF),
            pltpu.VMEM((2 * ROWS, D), BF),
            pltpu.VMEM((PLANES, ROWS, D), BF),
            dma((SEQ,)), dma((SEQ,)), dma((CHIPS,)), dma, dma, dma,
            dma((4,)), dma((4,)), dma((2,)), dma, dma, dma,
        ],
        compiler_params=pltpu.CompilerParams(
            collective_id=0, has_side_effects=True, vmem_limit_bytes=48 << 20),
    )(queries, keys, values, out_grad, out_weight)


def tail_kernel(ot_ref, dq_ref, dkv_ref, both_ref, dq_out, dkv_out, wo_out,
                o_buf, own_buf, *rest):
    bufs = [rest[6 * t:6 * t + 6] for t in range(3)]
    (o_send, dq_send, dkv_send, o_recv, dq_recv, dkv_recv, step_send, step_recv,
     wo_send, wo_recv, wo_own, pass_send, pass_recv) = rest[18:]
    plane, member, chip, core, x, y = position()
    entry_barrier(plane, member)
    target = lax.rem(lax.div(member, SIDE), 2)
    slot = lax.div(member, 2 * SIDE) * SIDE + lax.rem(member, SIDE)

    def o_copy(q):
        at = pl.ds(pl.multiple_of(q * 2 * ROWS, 2 * ROWS), 2 * ROWS)
        return ot_ref.at[:, at], o_buf.at[slot]

    @pl.loop(0, CHIPS)
    def _(k):
        q = lax.rem(chip + k, CHIPS)
        to = q * 2 + target
        src, dst = o_copy(q)

        @pl.when(to != member)
        def _():
            remote(src, dst, o_send.at[q], o_recv, seq=to).start()

        @pl.when(to == member)
        def _():
            local(src, dst, o_recv).start()

    local(dq_ref.at[member], dq_out.at[member], dq_recv).start()
    local(dkv_ref.at[member], dkv_out.at[member], dkv_recv).start()

    @pl.loop(1, SEQ)
    def _(k):
        to = lax.rem(member + k, SEQ)
        remote(dkv_ref.at[to], dkv_out.at[member], dkv_send.at[to], dkv_recv, seq=to).start()
        remote(dq_ref.at[to], dq_out.at[member], dq_send.at[to], dq_recv, seq=to).start()

    local(o_buf, o_buf, o_recv).wait()

    def place(part, zq, value, at):
        buf = bufs[part][0]
        if part == 0:
            buf[zq, :, at] = value
            return
        for xq in range(SIDE):
            for yq in range(SIDE):
                piece = value[(xq * SIDE + yq) * 16:(xq * SIDE + yq + 1) * 16]
                if part == 1:
                    buf[xq, pl.ds(pl.multiple_of(yq * 64 + zq * 16, 16), 16), at] = piece
                else:
                    buf[yq, pl.ds(pl.multiple_of(zq * 64 + xq * 16, 16), 16), at] = piece

    axes = (("fsdp", plane), ("x", x), ("y", y))
    orders = ((0, 1, 2), (1, 2, 0), (2, 0, 1))

    def steps(part, stage):
        name, here = axes[orders[part][stage]]
        send_buf, recv_buf = bufs[part][2 * stage], bufs[part][2 * stage + 1]
        copies = []
        for k in range(1, SIDE):
            there = lax.rem(here + k, SIDE)
            if name == "fsdp":
                where = dict(fsdp=there)
            elif name == "x":
                where = dict(seq=(there * SIDE + y) * 2 + core)
            else:
                where = dict(seq=(x * SIDE + there) * 2 + core)
            copies.append(remote(
                send_buf.at[there], recv_buf.at[here],
                step_send.at[part, stage, k - 1], step_recv.at[part, stage, k - 1], **where))
        return copies, here, send_buf, recv_buf

    def start(part, stage):
        for copy in steps(part, stage)[0]:
            copy.start()

    def multiply(tiles, parts_of):
        @pl.loop(0, PLANES)
        def _(zq):
            lhs = o_buf[pl.ds(zq * SIDE, SIDE)].reshape(ROWS, 2 * ROWS)
            for tile in tiles:
                value = jnp.dot(
                    lhs, both_ref[:, tile * ROWS:(tile + 1) * ROWS],
                    preferred_element_type=F32).astype(BF)
                for half in range(2):
                    col = tile * ROWS + half * BLK
                    for part in parts_of:
                        base, width = PARTS[part]
                        if base <= col < base + width:
                            place(part, zq, value[:, half * BLK:(half + 1) * BLK],
                                  slice(col - base, col - base + BLK))

    multiply((0, 1, 2), (0,))
    start(0, 0)
    multiply((3, 4, 5), (1, 2))
    start(1, 0)
    multiply((6, 7), (2,))
    start(2, 0)

    for stage in range(3):
        for part in range(3):
            copies, here, send_buf, recv_buf = steps(part, stage)
            for copy in copies:
                copy.wait_recv()
            base, width = PARTS[part]
            rows = send_buf.shape[1]
            total = None
            for piece in range(max(1, rows // 64)):
                count = min(rows, 64)
                at = pl.ds(piece * count, count)
                total = send_buf[here, at, :].astype(F32)
                for k in range(1, SIDE):
                    total = total + recv_buf[lax.rem(here + k, SIDE), at, :].astype(F32)
                if stage == 2:
                    own_buf[:, base:base + width] = total.astype(BF)
                else:
                    next_buf = bufs[part][2 * stage + 2]
                    if rows == 256:
                        next_buf[piece] = total.astype(BF)
                    else:
                        for t in range(SIDE):
                            next_buf[t] = total[t * 16:(t + 1) * 16].astype(BF)
            if stage < 2:
                start(part, stage + 1)

    def wo_rows(which, q):
        return wo_out.at[pl.ds(pl.multiple_of((which * CHIPS + q) * 16, 16), 16)]

    sibling = chip * 2 + 1 - core
    own = local(own_buf, wo_rows(core, chip), wo_own)
    own.start()

    @pl.loop(1, CHIPS)
    def _(k):
        q = lax.rem(chip + k, CHIPS)
        remote(own_buf, wo_rows(core, chip), wo_send.at[q], wo_recv.at[chip], seq=q * 2 + core).start()

    first = remote(own_buf, wo_rows(core, chip), pass_send.at[chip], pass_recv, seq=sibling)
    first.start()

    @pl.loop(1, CHIPS)
    def _(k):
        q = lax.rem(chip + CHIPS - k, CHIPS)
        remote(own_buf, wo_rows(core, q), wo_send.at[q], wo_recv.at[q], seq=q * 2 + core).wait_recv()
        remote(wo_rows(core, q), wo_rows(core, q), pass_send.at[q], pass_recv, seq=sibling).start()

    own.wait()
    other = pl.ds(pl.multiple_of((1 - core) * ROWS, ROWS), ROWS)
    local(wo_out.at[other], wo_out.at[other], pass_recv).wait()
    first.wait_send()

    @pl.loop(1, CHIPS)
    def _(k):
        q = lax.rem(chip + k, CHIPS)
        remote(own_buf, wo_rows(core, chip), wo_send.at[q], wo_recv.at[chip], seq=q * 2 + core).wait_send()
        remote(wo_rows(core, q), wo_rows(core, q), pass_send.at[q], pass_recv, seq=sibling).wait_send()

    @pl.loop(0, CHIPS)
    def _(q):
        to = q * 2 + target
        src, dst = o_copy(q)

        @pl.when(to != member)
        def _():
            remote(src, dst, o_send.at[q], o_recv, seq=to).wait_send()

    for stage in range(3):
        for part in range(3):
            for copy in steps(part, stage)[0]:
                copy.wait_send()

    @pl.loop(1, SEQ)
    def _(k):
        to = lax.rem(member + k, SEQ)
        remote(dkv_ref.at[to], dkv_out.at[member], dkv_send.at[to], dkv_recv, seq=to).wait_send()
        remote(dq_ref.at[to], dq_out.at[member], dq_send.at[to], dq_recv, seq=to).wait_send()

    local(dkv_out, dkv_out, dkv_recv).wait()
    local(dq_out, dq_out, dq_recv).wait()


def tail_exchange(ot, dq, dkv, both):
    anyway = pl.BlockSpec(memory_space=pl.ANY)
    whole = pl.BlockSpec(memory_space=pltpu.VMEM)
    dma = pltpu.SemaphoreType.DMA
    stages = []
    for _, width in PARTS:
        for rows in (256, 64, 16):
            stages += [pltpu.VMEM((SIDE, rows, width), BF)] * 2
    return pl.pallas_call(
        tail_kernel,
        out_shape=(
            jax.ShapeDtypeStruct((SEQ, BLK, 2 * HD), BF),
            jax.ShapeDtypeStruct((SEQ, ROWS, 2 * HD), BF),
            jax.ShapeDtypeStruct((2 * ROWS, D), BF),
        ),
        in_specs=[anyway, anyway, anyway, whole],
        out_specs=(anyway, anyway, anyway),
        scratch_shapes=[
            pltpu.VMEM((CHIPS, HD, 2 * ROWS), BF),
            pltpu.VMEM((16, D), BF),
            *stages,
            dma((CHIPS,)), dma((SEQ,)), dma((SEQ,)), dma, dma, dma,
            dma((3, 3, 3)), dma((3, 3, 3)),
            dma((CHIPS,)), dma((CHIPS,)), dma, dma((CHIPS,)), dma,
        ],
        compiler_params=pltpu.CompilerParams(
            collective_id=1, has_side_effects=True, vmem_limit_bytes=48 << 20),
    )(ot, dq, dkv, both)


def finish_kernel(dq_ref, dkv_ref, wo_ref, dq_out, dk_out, dv_out, wo_out):
    for j in range(HEADS // 2):
        at = slice(j * 2 * HD, (j + 1) * 2 * HD)
        one, two = dkv_ref[2 * j], dkv_ref[2 * j + 1]
        dk_out[:, at], dv_out[:, at] = halves(one, two)
        one, two = dq_ref[2 * j], dq_ref[2 * j + 1]
        dq_out[:BLK, at], dq_out[BLK:, at] = halves(one, two)
    for r in range(8):
        at = slice(r * 64, (r + 1) * 64)
        wo_out[at, :] = wo_ref[at, :].astype(F32)


def finish(dq, dkv, wo):
    whole = pl.BlockSpec(memory_space=pltpu.VMEM)
    shape = jax.ShapeDtypeStruct((ROWS, D), BF)
    return pl.pallas_call(
        finish_kernel,
        out_shape=(shape, shape, shape, jax.ShapeDtypeStruct(wo.shape, F32)),
        in_specs=[whole] * 3,
        out_specs=(whole,) * 4,
        compiler_params=pltpu.CompilerParams(vmem_limit_bytes=48 << 20),
    )(dq, dkv, wo)


def attention_kernel(adj_ref, count_ref, q_ref, g_ref, kv_ref, dq_ref, ot_ref, dkv_ref,
                     qg_ref, acc_ref, kvt_ref, dqt_ref, sd_ref, te_ref):
    blocks = kv_ref.shape[0] // BLK
    first = lax.broadcasted_iota(jnp.int32, (BLK, BLK), 1) < HD
    half_scale = jnp.where(first, HD ** -0.5, 1.0).astype(F32)
    score_scale = HD ** -0.5 * LOG2E

    def rows(b):
        return pl.ds(pl.multiple_of(b * BLK, BLK), BLK)

    def swap(value):
        return jnp.concatenate([value[:, HD:], value[:, :HD]], axis=1)

    @pl.loop(0, blocks)
    def _(b):
        acc_ref[rows(b), :] = jnp.zeros((BLK, BLK), F32)
        kvt_ref[rows(b), :] = kv_ref[rows(b), :].T

    @pl.loop(0, blocks // 2)
    def _(b):
        q, g = q_ref[rows(b), :], g_ref[rows(b), :]
        qg_ref[rows(2 * b), :] = jnp.where(first, q, swap(g))
        qg_ref[rows(2 * b + 1), :] = jnp.where(first, swap(q), g)

    def fold(value, op):
        parts = [value[r * 8:(r + 1) * 8] for r in range(value.shape[0] // 8)]
        while len(parts) > 1:
            parts = [op(parts[t], parts[t + 1]) for t in range(0, len(parts) - 1, 2)] + (
                [parts[-1]] if len(parts) % 2 else [])
        return parts[0]

    def one_block(i, n):
        qg = qg_ref[rows(i), :]
        zero = jnp.zeros_like(qg)
        pair = jnp.concatenate([jnp.where(first, qg, zero), jnp.where(first, zero, qg)], axis=0)
        picked = [adj_ref[i, j] for j in range(n)]
        top = None
        for j in range(n):
            sd = lax.dot_general(
                kv_ref[rows(picked[j]), :], pair, (((1,), (1,)), ((), ())),
                preferred_element_type=F32)
            sd_ref[j * BLK:(j + 1) * BLK, :] = sd
            part = fold(sd[:, :BLK], jnp.maximum)
            top = part if top is None else jnp.maximum(top, part)
        top = jnp.max(top, axis=0, keepdims=True) * score_scale
        total = None
        dots = None
        for j in range(n):
            at = slice(j * BLK, (j + 1) * BLK)
            expo = jnp.exp2(sd_ref[at, :BLK] * score_scale - top)
            sd_ref[at, :BLK] = expo
            part = fold(expo, jnp.add)
            total = part if total is None else total + part
            part = fold(expo * sd_ref[at, BLK:], jnp.add)
            dots = part if dots is None else dots + part
        inv = 1.0 / jnp.sum(total, axis=0, keepdims=True)
        row_dot = jnp.sum(dots, axis=0, keepdims=True) * inv
        for j in range(n):
            at = slice(j * BLK, (j + 1) * BLK)
            prob = sd_ref[at, :BLK] * inv
            grad = prob * (sd_ref[at, BLK:] - row_dot)
            te = jnp.concatenate([grad.astype(BF), prob.astype(BF)], axis=1)
            te_ref[at, :] = te
            acc_ref[rows(picked[j]), :] += jnp.dot(te, pair, preferred_element_type=F32)
        kvt = jnp.concatenate([kvt_ref[rows(picked[j]), :] for j in range(n)], axis=1)
        out = jnp.dot(kvt, te_ref[:n * BLK, :], preferred_element_type=F32)
        dqt_ref[pl.ds(pl.multiple_of(i * HD, HD), HD), :] = out[:HD, :BLK] * HD ** -0.5
        ot_ref[:, rows(i)] = out[HD:, BLK:].astype(BF)

    @pl.loop(0, blocks)
    def _(i):
        count = count_ref[i]
        for n in range(2, MAXK + 1):
            @pl.when(count == n)
            def _():
                one_block(i, n)

    @pl.loop(0, blocks)
    def _(b):
        dkv_ref[rows(b), :] = (acc_ref[rows(b), :] * half_scale).astype(BF)

    @pl.loop(0, blocks // 2)
    def _(b):
        dq_ref[rows(b), :] = dqt_ref[rows(b), :].T.astype(BF)


def attention(adjacency, counts, q, g, kv):
    tokens = kv.shape[0]
    whole = pl.BlockSpec(memory_space=pltpu.VMEM)
    scalar = pl.BlockSpec(memory_space=pltpu.SMEM)
    return pl.pallas_call(
        attention_kernel,
        out_shape=(
            jax.ShapeDtypeStruct((tokens // 2, 2 * HD), BF),
            jax.ShapeDtypeStruct((HD, tokens), BF),
            jax.ShapeDtypeStruct((tokens, 2 * HD), BF),
        ),
        in_specs=[scalar, scalar, whole, whole, whole],
        out_specs=(whole, whole, whole),
        scratch_shapes=[
            pltpu.VMEM((tokens, 2 * HD), BF),
            pltpu.VMEM((tokens, 2 * HD), F32),
            pltpu.VMEM((tokens, 2 * HD), BF),
            pltpu.VMEM((tokens // 2, 2 * HD), F32),
            pltpu.VMEM((MAXK * BLK, 2 * BLK), F32),
            pltpu.VMEM((MAXK * BLK, 2 * BLK), BF),
        ],
        compiler_params=pltpu.CompilerParams(vmem_limit_bytes=48 << 20),
    )(adjacency, counts, q, g, kv)


def on_device(queries, keys, values, out_grad, out_weight, key_blocks, block_counts):
    q, kv, g, both = head_exchange(queries[0], keys[0], values[0], out_grad[0], out_weight)
    dq, ot, dkv = attention(
        key_blocks[0], block_counts[0], q.reshape(-1, 2 * HD), g.reshape(-1, 2 * HD),
        kv.reshape(-1, 2 * HD))
    dq, dkv, wo = tail_exchange(
        ot, dq.reshape(SEQ, BLK, 2 * HD), dkv.reshape(SEQ, ROWS, 2 * HD), both)
    query_grad, key_grad, value_grad, wo_grad = finish(dq, dkv, wo)
    return (query_grad[None], key_grad[None], value_grad[None], wo_grad)


def solution(mesh):
    return jax.shard_map(
        on_device,
        mesh=mesh,
        in_specs=(
            P("fsdp", "seq", None),
            P("fsdp", "seq", None),
            P("fsdp", "seq", None),
            P("fsdp", "seq", None),
            P("fsdp", None),
            P("fsdp", None, None),
            P("fsdp", None),
        ),
        out_specs=(
            P("fsdp", "seq", None),
            P("fsdp", "seq", None),
            P("fsdp", "seq", None),
            P("fsdp", None),
        ),
        check_vma=False,
    )
```

time: 436 us -> 290 us (0.67)
  Pallas kernels: 80.2 us -> 283 us
  blocking collectives: 175 us -> 0 us
  waiting for transfers between devices: 116 us -> 0 us
  starting transfers between devices: 16.3 us -> 0 us
  matrix products: 13.6 us -> 0 us
  between operations: 14.1 us -> 0.67 us
  other arithmetic: 10.3 us -> 0 us
    pallas_call x5 -> x4, Pallas kernels: 80.2 us -> 283 us  [the longest x1 147 us: tail_exchange(): pl.pallas_call(tail_kernel, out_shape=(jax.ShapeDtypeStruct((SEQ, BLK, 2...]
    all_to_all x4 -> x0, blocking collectives: 175 us -> none  [the longest x1 100 us: on_device(): term = lax.all_to_all(term, 'seq', split_axis=0, concat_axis=0, tiled=True)]
    all_gather x2 -> x0, waiting for transfers between devices: 87.1 us -> none  [the longest x1 76.2 us: on_device(): lax.all_gather(out_weight, 'fsdp', axis=0, tiled=True)]
    all_to_all x2 -> x0, waiting for transfers between devices: 28.2 us -> none  [exchange(): lax.all_to_all(packed, 'seq', split_axis=0, concat_axis=0, tiled=True)]
    all_to_all x2 -> x0, starting transfers between devices: 16.2 us -> none  [exchange(): lax.all_to_all(packed, 'seq', split_axis=0, concat_axis=0, tiled=True)]
    dot_general x2 -> x0, matrix products: 13.6 us -> none  [the longest x1 6.84 us: on_device(): lax.dot_general(attn_out, loss_grad, (((0,), (0,)), ((), ())), preferred_...]
    reshape x1 -> x0, local copies, waits for them, and re-layouts: 8.26 us -> none  [on_device(): term.reshape(planes, parts, width // planes // parts, width)]
    reduce_sum x2 -> x0, other arithmetic: 6.2 us -> none  [the longest x1 5.53 us: on_device(): term = jnp.sum(term.astype(jnp.float32), axis=0).astype(jnp.bfloat16)]
  transfers between devices with their start and end apart: 4 -> 0, of which waited for: 3 -> 0; matrix products, arithmetic and copies ran while one was open for 2% -> 0% of each run, Pallas kernels for 2% -> 0%
where the time goes in v2:
time: 290 us
  Pallas kernels  283 us (98%)
  local copies, waits for them, and re-layouts  6.04 us (2%)
    pallas_call x1, Pallas kernels, tail_exchange(): pl.pallas_call(tail_kernel, out_shape=(jax.ShapeDtypeStruct((SEQ, BLK, 2...  147 us
    pallas_call x1, Pallas kernels, head_exchange(): pl.pallas_call(head_kernel, out_shape=(jax.ShapeDtypeStruct((SEQ, BLK, 2...  67.8 us
    pallas_call x1, Pallas kernels, attention(): pl.pallas_call(attention_kernel, out_shape=(jax.ShapeDtypeStruct((tokens...  63.9 us
    unnamed x11, local copies, waits for them, and re-layouts  6.04 us

profile of v2, /device:TPU:1, one launch (start us, length us, event | category | flops | bytes accessed | tf_op | source)
XLA Modules:
  0.0 289.9 jit_solution(17970949270809403599)
XLA Ops:
  0.6 0.8 copy.11
  1.4 0.0 copy-start.1
  1.4 1.2 copy-done.1
  2.6 0.0 copy-start.2
  2.6 1.2 copy-done.2
  3.9 0.0 copy-start.3
  3.9 1.2 copy-done.3
  5.1 0.0 copy-start.4
  5.1 67.8 %shard_map.102 = (bf16[32,128,128]{2,1,0:T(8,128)(2,1)S(1)}, bf16[32,256,128]{2,1,0:T(8,128)(2,1)}, bf16[16,256,128]{2,1,0:T(8,128)(2,1)S(1)}, bf16[512,2048]{1,0:T(8,128)(2,1)}) custom-call(bf16[256,2048]{1,0:T(8,128)(2,1)S(1)} %bitcast.16, bf16[256,2048]{1,0:T(8,128)(2,1)S(1)} %bitcast.17, bf16[256,2048]{1,0:T(8,128)(2,1)S(1)} %bitcast.18, ...), custom_call_target="tpu_custom_call" | custom-call | tf_op jit(solution)/shard_map/pallas_call | solution.py:170
  72.9 0.0 copy-done.4
  72.9 63.9 %shard_map.103 = (bf16[4096,128]{1,0:T(8,128)(2,1)S(1)}, bf16[64,8192]{1,0:T(8,128)(2,1)S(1)}, bf16[8192,128]{1,0:T(8,128)(2,1)}) custom-call(s32[64,10]{1,0:T(8,128)S(1)} %bitcast.20, s32[64]{0:T(128)S(1)} %bitcast.21, bf16[4096,128]{1,0:T(8,128)(2,1)S(1)} %bitcast.14, bf16[4096,128]{1,0:T(8,128)(2,1)S(1)} %bitcast.15, bf16[8192,128]{1,0:T(8,128)(2,1)} %bitcast.23), custom_call_target="tpu_custom_call" | custom-call | tf_op jit(solution)/shard_map/pallas_call | solution.py:519
  136.8 147.4 %shard_map.104 = (bf16[32,128,128]{2,1,0:T(8,128)(2,1)S(1)}, bf16[32,256,128]{2,1,0:T(8,128)(2,1)S(1)}, bf16[512,2048]{1,0:T(8,128)(2,1)}) custom-call(bf16[64,8192]{1,0:T(8,128)(2,1)S(1)} %get-tuple-element.21.ot_ref, bf16[32,128,128]{2,1,0:T(8,128)(2,1)S(1)} %bitcast.19, bf16[32,256,128]{2,1,0:T(8,128)(2,1)} %bitcast.22, ...), custom_call_target="tpu_custom_call" | custom-call | tf_op jit(solution)/shard_map/pallas_call | solution.py:383
  284.2 0.0 copy-start
  284.3 1.6 copy-done
  285.8 4.1 %shard_map.105 = (bf16[256,2048]{1,0:T(8,128)(2,1)}, bf16[256,2048]{1,0:T(8,128)(2,1)}, bf16[256,2048]{1,0:T(8,128)(2,1)}, f32[512,2048]{1,0:T(8,128)}) custom-call(bf16[32,128,128]{2,1,0:T(8,128)(2,1)S(1)} %get-tuple-element.25.dq_ref, bf16[32,256,128]{2,1,0:T(8,128)(2,1)S(1)} %get-tuple-element.26.dkv_ref, bf16[512,2048]{1,0:T(8,128)(2,1)S(1)} %copy-done), custom_call_target="tpu_custom_call" | custom-call | tf_op jit(solution)/shard_map/pallas_call | solution.py:420
Async XLA Ops:
  1.4 1.2 copy-start.1
  2.6 1.2 copy-start.2
  3.9 1.2 copy-start.3
  5.1 67.8 %copy-start.4 = (s32[1,64]{1,0:T(1,128)S(1)}, s32[1,64]{1,0:T(1,128)}, u32[]{:S(2)}) copy-start(s32[1,64]{1,0:T(1,128)} %param.13) | copy-start | bytes 772
  284.2 1.6 copy-start

commit v3 on v2

--- a/solution.py
+++ b/solution.py
@@ -9,6 +9,8 @@
 HD = 64
 BLK = 128
 MAXK = 10
+NBLK = 64
+GROUP = 2
 LOG2E = 1.4426950408889634
 SEQ = 32
 SIDE = 4
@@ -18,6 +20,7 @@
 ROWS = 256
 BF = jnp.bfloat16
 F32 = jnp.float32
+GROUPS = (10, 22, 28, 32)
 PARTS = ((0, 768), (768, 640), (1408, 640))
 
 
@@ -53,6 +56,15 @@
             device_id_type=pl.DeviceIdType.MESH)
 
     pl.semaphore_wait(barrier, SEQ + PLANES - 2)
+
+
+def owner(head):
+    quarter, core, x = head // 8, head // SIDE % 2, head % SIDE
+    return (x * SIDE + (x + quarter) % SIDE) * 2 + core
+
+
+def traced_owner(quarter, core, x):
+    return (x * SIDE + lax.rem(x + quarter, SIDE)) * 2 + core
 
 
 def halves(one, two):
@@ -95,23 +107,28 @@
         def _():
             remote(block, out.at[slot], send_sem, recv_sem, seq=head).wait_send()
 
+    def pair_owner(j, e):
+        return traced_owner(lax.div(j, 4), lax.rem(lax.div(j, 2), 2), lax.rem(j, 2) * 2 + e)
+
     @pl.loop(0, CHIPS)
     def _(k):
-        j = lax.rem(chip + k, CHIPS)
+        j = lax.rem(chip + 5 * k, CHIPS)
         at = pl.ds(pl.multiple_of(j * 2 * HD, 2 * HD), 2 * HD)
         kv = halves(k_ref[:, at], v_ref[:, at])
         for e in range(2):
-            kv_pack[2 * j + e] = kv[e]
-            send(kv_pack.at[2 * j + e], 2 * j + e, kv_out, member, kv_send.at[2 * j + e], kv_recv)
+            to = pair_owner(j, e)
+            kv_pack[to] = kv[e]
+            send(kv_pack.at[to], to, kv_out, member, kv_send.at[to], kv_recv)
 
     @pl.loop(0, CHIPS)
     def _(k):
-        j = lax.rem(chip + k, CHIPS)
+        j = lax.rem(chip + 5 * k, CHIPS)
         at = pl.ds(pl.multiple_of(j * 2 * HD, 2 * HD), 2 * HD)
         q = halves(q_ref[:BLK, at], q_ref[BLK:, at])
         for e in range(2):
-            q_pack[2 * j + e] = q[e]
-            send(q_pack.at[2 * j + e], 2 * j + e, q_out, member, q_send.at[2 * j + e], q_recv)
+            to = pair_owner(j, e)
+            q_pack[to] = q[e]
+            send(q_pack.at[to], to, q_out, member, q_send.at[to], q_recv)
 
     def project(which):
         for pair in range(2):
@@ -122,7 +139,7 @@
             low = halves(grad[2 * BLK:3 * BLK], grad[3 * BLK:])
             for e in range(2):
                 slot = which * SIDE + pair * 2 + e
-                head = which * 2 * SIDE + core * SIDE + pair * 2 + e
+                head = traced_owner(which, core, pair * 2 + e)
                 g_pack[slot, :BLK, :] = top[e]
                 g_pack[slot, BLK:, :] = low[e]
                 send(g_pack.at[slot], head, g_out, chip, g_send.at[slot], g_recv)
@@ -155,7 +172,7 @@
 
     @pl.loop(0, CHIPS)
     def _(slot):
-        head = lax.div(slot, SIDE) * 2 * SIDE + core * SIDE + lax.rem(slot, SIDE)
+        head = traced_owner(lax.div(slot, SIDE), core, lax.rem(slot, SIDE))
         sent(g_pack.at[slot], head, g_out, chip, g_send.at[slot], g_recv)
 
     local(kv_out, kv_out, kv_recv).wait()
@@ -198,8 +215,7 @@
      wo_send, wo_recv, wo_own, pass_send, pass_recv) = rest[18:]
     plane, member, chip, core, x, y = position()
     entry_barrier(plane, member)
-    target = lax.rem(lax.div(member, SIDE), 2)
-    slot = lax.div(member, 2 * SIDE) * SIDE + lax.rem(member, SIDE)
+    slot = lax.rem(y + SIDE - x, SIDE) * SIDE + x
 
     def o_copy(q):
         at = pl.ds(pl.multiple_of(q * 2 * ROWS, 2 * ROWS), 2 * ROWS)
@@ -207,8 +223,8 @@
 
     @pl.loop(0, CHIPS)
     def _(k):
-        q = lax.rem(chip + k, CHIPS)
-        to = q * 2 + target
+        q = lax.rem(chip + 5 * k, CHIPS)
+        to = q * 2 + core
         src, dst = o_copy(q)
 
         @pl.when(to != member)
@@ -222,12 +238,14 @@
     local(dq_ref.at[member], dq_out.at[member], dq_recv).start()
     local(dkv_ref.at[member], dkv_out.at[member], dkv_recv).start()
 
-    @pl.loop(1, SEQ)
-    def _(k):
-        to = lax.rem(member + k, SEQ)
-        remote(dkv_ref.at[to], dkv_out.at[member], dkv_send.at[to], dkv_recv, seq=to).start()
-        remote(dq_ref.at[to], dq_out.at[member], dq_send.at[to], dq_recv, seq=to).start()
-
+    def group(low, high):
+        @pl.loop(low, high)
+        def _(k):
+            to = lax.rem(member + 9 * k, SEQ)
+            remote(dkv_ref.at[to], dkv_out.at[member], dkv_send.at[to], dkv_recv, seq=to).start()
+            remote(dq_ref.at[to], dq_out.at[member], dq_send.at[to], dq_recv, seq=to).start()
+
+    group(1, GROUPS[0])
     local(o_buf, o_buf, o_recv).wait()
 
     def place(part, zq, value, at):
@@ -289,6 +307,7 @@
     start(1, 0)
     multiply((6, 7), (2,))
     start(2, 0)
+    group(GROUPS[0], GROUPS[1])
 
     for stage in range(3):
         for part in range(3):
@@ -315,6 +334,8 @@
                             next_buf[t] = total[t * 16:(t + 1) * 16].astype(BF)
             if stage < 2:
                 start(part, stage + 1)
+        if stage < 2:
+            group(GROUPS[stage + 1], GROUPS[stage + 2])
 
     def wo_rows(which, q):
         return wo_out.at[pl.ds(pl.multiple_of((which * CHIPS + q) * 16, 16), 16)]
@@ -325,7 +346,7 @@
 
     @pl.loop(1, CHIPS)
     def _(k):
-        q = lax.rem(chip + k, CHIPS)
+        q = lax.rem(chip + 5 * k, CHIPS)
         remote(own_buf, wo_rows(core, chip), wo_send.at[q], wo_recv.at[chip], seq=q * 2 + core).start()
 
     first = remote(own_buf, wo_rows(core, chip), pass_send.at[chip], pass_recv, seq=sibling)
@@ -333,7 +354,7 @@
 
     @pl.loop(1, CHIPS)
     def _(k):
-        q = lax.rem(chip + CHIPS - k, CHIPS)
+        q = lax.rem(chip + 11 * k, CHIPS)
         remote(own_buf, wo_rows(core, q), wo_send.at[q], wo_recv.at[q], seq=q * 2 + core).wait_recv()
         remote(wo_rows(core, q), wo_rows(core, q), pass_send.at[q], pass_recv, seq=sibling).start()
 
@@ -350,7 +371,7 @@
 
     @pl.loop(0, CHIPS)
     def _(q):
-        to = q * 2 + target
+        to = q * 2 + core
         src, dst = o_copy(q)
 
         @pl.when(to != member)
@@ -405,9 +426,9 @@
 def finish_kernel(dq_ref, dkv_ref, wo_ref, dq_out, dk_out, dv_out, wo_out):
     for j in range(HEADS // 2):
         at = slice(j * 2 * HD, (j + 1) * 2 * HD)
-        one, two = dkv_ref[2 * j], dkv_ref[2 * j + 1]
+        one, two = dkv_ref[owner(2 * j)], dkv_ref[owner(2 * j + 1)]
         dk_out[:, at], dv_out[:, at] = halves(one, two)
-        one, two = dq_ref[2 * j], dq_ref[2 * j + 1]
+        one, two = dq_ref[owner(2 * j)], dq_ref[owner(2 * j + 1)]
         dq_out[:BLK, at], dq_out[BLK:, at] = halves(one, two)
     for r in range(8):
         at = slice(r * 64, (r + 1) * 64)
@@ -427,7 +448,7 @@
 
 
 def attention_kernel(adj_ref, count_ref, q_ref, g_ref, kv_ref, dq_ref, ot_ref, dkv_ref,
-                     qg_ref, acc_ref, kvt_ref, dqt_ref, sd_ref, te_ref):
+                     qg_ref, acc_ref, kvt_ref, dqt_ref, sd_ref, te_ref, list_ref, size_ref):
     blocks = kv_ref.shape[0] // BLK
     first = lax.broadcasted_iota(jnp.int32, (BLK, BLK), 1) < HD
     half_scale = jnp.where(first, HD ** -0.5, 1.0).astype(F32)
@@ -439,16 +460,27 @@
     def swap(value):
         return jnp.concatenate([value[:, HD:], value[:, :HD]], axis=1)
 
+    @pl.loop(0, blocks // 8)
+    def _(s):
+        for t in range(8):
+            b = s * 8 + t
+            acc_ref[rows(b), :] = jnp.zeros((BLK, BLK), F32)
+            kvt_ref[rows(b), :] = kv_ref[rows(b), :].T
+        for t in range(4):
+            b = s * 4 + t
+            q, g = q_ref[rows(b), :], g_ref[rows(b), :]
+            qg_ref[rows(2 * b), :] = jnp.where(first, q, swap(g))
+            qg_ref[rows(2 * b + 1), :] = jnp.where(first, swap(q), g)
+
+    for n in range(MAXK + 1):
+        size_ref[n] = 0
+
     @pl.loop(0, blocks)
-    def _(b):
-        acc_ref[rows(b), :] = jnp.zeros((BLK, BLK), F32)
-        kvt_ref[rows(b), :] = kv_ref[rows(b), :].T
-
-    @pl.loop(0, blocks // 2)
-    def _(b):
-        q, g = q_ref[rows(b), :], g_ref[rows(b), :]
-        qg_ref[rows(2 * b), :] = jnp.where(first, q, swap(g))
-        qg_ref[rows(2 * b + 1), :] = jnp.where(first, swap(q), g)
+    def _(i):
+        count = count_ref[i]
+        filled = size_ref[count]
+        list_ref[count, filled] = i
+        size_ref[count] = filled + 1
 
     def fold(value, op):
         parts = [value[r * 8:(r + 1) * 8] for r in range(value.shape[0] // 8)]
@@ -457,59 +489,75 @@
                 [parts[-1]] if len(parts) % 2 else [])
         return parts[0]
 
-    def one_block(i, n):
-        qg = qg_ref[rows(i), :]
-        zero = jnp.zeros_like(qg)
-        pair = jnp.concatenate([jnp.where(first, qg, zero), jnp.where(first, zero, qg)], axis=0)
-        picked = [adj_ref[i, j] for j in range(n)]
-        top = None
-        for j in range(n):
-            sd = lax.dot_general(
-                kv_ref[rows(picked[j]), :], pair, (((1,), (1,)), ((), ())),
-                preferred_element_type=F32)
-            sd_ref[j * BLK:(j + 1) * BLK, :] = sd
-            part = fold(sd[:, :BLK], jnp.maximum)
-            top = part if top is None else jnp.maximum(top, part)
-        top = jnp.max(top, axis=0, keepdims=True) * score_scale
-        total = None
-        dots = None
-        for j in range(n):
-            at = slice(j * BLK, (j + 1) * BLK)
-            expo = jnp.exp2(sd_ref[at, :BLK] * score_scale - top)
-            sd_ref[at, :BLK] = expo
-            part = fold(expo, jnp.add)
-            total = part if total is None else total + part
-            part = fold(expo * sd_ref[at, BLK:], jnp.add)
-            dots = part if dots is None else dots + part
-        inv = 1.0 / jnp.sum(total, axis=0, keepdims=True)
-        row_dot = jnp.sum(dots, axis=0, keepdims=True) * inv
-        for j in range(n):
-            at = slice(j * BLK, (j + 1) * BLK)
-            prob = sd_ref[at, :BLK] * inv
-            grad = prob * (sd_ref[at, BLK:] - row_dot)
-            te = jnp.concatenate([grad.astype(BF), prob.astype(BF)], axis=1)
-            te_ref[at, :] = te
-            acc_ref[rows(picked[j]), :] += jnp.dot(te, pair, preferred_element_type=F32)
-        kvt = jnp.concatenate([kvt_ref[rows(picked[j]), :] for j in range(n)], axis=1)
-        out = jnp.dot(kvt, te_ref[:n * BLK, :], preferred_element_type=F32)
-        dqt_ref[pl.ds(pl.multiple_of(i * HD, HD), HD), :] = out[:HD, :BLK] * HD ** -0.5
-        ot_ref[:, rows(i)] = out[HD:, BLK:].astype(BF)
-
-    @pl.loop(0, blocks)
-    def _(i):
-        count = count_ref[i]
-        for n in range(2, MAXK + 1):
-            @pl.when(count == n)
-            def _():
-                one_block(i, n)
-
-    @pl.loop(0, blocks)
-    def _(b):
-        dkv_ref[rows(b), :] = (acc_ref[rows(b), :] * half_scale).astype(BF)
-
-    @pl.loop(0, blocks // 2)
-    def _(b):
-        dq_ref[rows(b), :] = dqt_ref[rows(b), :].T.astype(BF)
+    def process(members, n):
+        pairs, picked = [], []
+        for i in members:
+            qg = qg_ref[rows(i), :]
+            zero = jnp.zeros_like(qg)
+            pairs.append(jnp.concatenate(
+                [jnp.where(first, qg, zero), jnp.where(first, zero, qg)], axis=0))
+            picked.append([adj_ref[i, j] for j in range(n)])
+        size = len(members)
+        slots = [slice(j * BLK, (j + 1) * BLK) for j in range(n)]
+        tops = []
+        for m in range(size):
+            top = None
+            for j in range(n):
+                sd = lax.dot_general(
+                    kv_ref[rows(picked[m][j]), :], pairs[m], (((1,), (1,)), ((), ())),
+                    preferred_element_type=F32)
+                sd_ref[m, slots[j], :] = sd
+                part = fold(sd[:, :BLK], jnp.maximum)
+                top = part if top is None else jnp.maximum(top, part)
+            tops.append(jnp.max(top, axis=0, keepdims=True) * score_scale)
+        invs, row_dots = [], []
+        for m in range(size):
+            total = dots = None
+            for j in range(n):
+                expo = jnp.exp2(sd_ref[m, slots[j], :BLK] * score_scale - tops[m])
+                sd_ref[m, slots[j], :BLK] = expo
+                part = fold(expo, jnp.add)
+                total = part if total is None else total + part
+                part = fold(expo * sd_ref[m, slots[j], BLK:], jnp.add)
+                dots = part if dots is None else dots + part
+            inv = 1.0 / jnp.sum(total, axis=0, keepdims=True)
+            invs.append(inv)
+            row_dots.append(jnp.sum(dots, axis=0, keepdims=True) * inv)
+        for m in range(size):
+            for j in range(n):
+                prob = sd_ref[m, slots[j], :BLK] * invs[m]
+                grad = prob * (sd_ref[m, slots[j], BLK:] - row_dots[m])
+                te = jnp.concatenate([grad.astype(BF), prob.astype(BF)], axis=1)
+                te_ref[m, slots[j], :] = te
+                acc_ref[rows(picked[m][j]), :] += jnp.dot(te, pairs[m], preferred_element_type=F32)
+        for m in range(size):
+            i = members[m]
+            kvt = jnp.concatenate([kvt_ref[rows(picked[m][j]), :] for j in range(n)], axis=1)
+            dq = jnp.dot(kvt[:HD], te_ref[m, :n * BLK, :BLK], preferred_element_type=F32)
+            out = jnp.dot(kvt[HD:], te_ref[m, :n * BLK, BLK:], preferred_element_type=F32)
+            dqt_ref[pl.ds(pl.multiple_of(i * HD, HD), HD), :] = dq * HD ** -0.5
+            ot_ref[:, rows(i)] = out.astype(BF)
+
+    for n in range(2, MAXK + 1):
+        size = size_ref[n]
+        whole = lax.div(size, GROUP)
+
+        @pl.loop(0, whole)
+        def _(t):
+            process([list_ref[n, t * GROUP + m] for m in range(GROUP)], n)
+
+        @pl.loop(whole * GROUP, size)
+        def _(t):
+            process([list_ref[n, t]], n)
+
+    @pl.loop(0, blocks // 8)
+    def _(s):
+        for t in range(8):
+            b = s * 8 + t
+            dkv_ref[rows(b), :] = (acc_ref[rows(b), :] * half_scale).astype(BF)
+        for t in range(4):
+            b = s * 4 + t
+            dq_ref[rows(b), :] = dqt_ref[rows(b), :].T.astype(BF)
 
 
 def attention(adjacency, counts, q, g, kv):
@@ -530,8 +578,10 @@
             pltpu.VMEM((tokens, 2 * HD), F32),
             pltpu.VMEM((tokens, 2 * HD), BF),
             pltpu.VMEM((tokens // 2, 2 * HD), F32),
-            pltpu.VMEM((MAXK * BLK, 2 * BLK), F32),
-            pltpu.VMEM((MAXK * BLK, 2 * BLK), BF),
+            pltpu.VMEM((GROUP, MAXK * BLK, 2 * BLK), F32),
+            pltpu.VMEM((GROUP, MAXK * BLK, 2 * BLK), BF),
+            pltpu.SMEM((MAXK + 1, NBLK), jnp.int32),
+            pltpu.SMEM((MAXK + 1,), jnp.int32),
         ],
         compiler_params=pltpu.CompilerParams(vmem_limit_bytes=48 << 20),
     )(adjacency, counts, q, g, kv)

time: 290 us -> 212 us (0.73)
  Pallas kernels: 283 us -> 204 us
    pallas_call x1, Pallas kernels: 147 us -> 100 us  [tail_exchange(): pl.pallas_call(tail_kernel, out_shape=(jax.ShapeDtypeStruct((SEQ, BLK, 2...]
    pallas_call x1, Pallas kernels: 63.9 us -> 39 us  [attention(): pl.pallas_call(attention_kernel, out_shape=(jax.ShapeDtypeStruct((tokens...]
    pallas_call x1, Pallas kernels: 67.8 us -> 60.9 us  [head_exchange(): pl.pallas_call(head_kernel, out_shape=(jax.ShapeDtypeStruct((SEQ, BLK, 2...]
where the time goes in v3:
time: 212 us; the launch traced here: 211 us
  Pallas kernels  204 us (96%)
  local copies, waits for them, and re-layouts  6.04 us (3%)
    pallas_call x1, Pallas kernels, tail_exchange(): pl.pallas_call(tail_kernel, out_shape=(jax.ShapeDtypeStruct((SEQ, BLK, 2...  100 us
    pallas_call x1, Pallas kernels, head_exchange(): pl.pallas_call(head_kernel, out_shape=(jax.ShapeDtypeStruct((SEQ, BLK, 2...  60.9 us
    pallas_call x1, Pallas kernels, attention(): pl.pallas_call(attention_kernel, out_shape=(jax.ShapeDtypeStruct((tokens...  39 us
    unnamed x11, local copies, waits for them, and re-layouts  6.04 us

profile of v3, /device:TPU:1, one launch (start us, length us, event | category | flops | bytes accessed | tf_op | source)
XLA Modules:
  0.0 211.0 jit_solution(11719106851150962000)
XLA Ops:
  0.6 0.8 copy.11
  1.4 0.0 copy-start.1
  1.4 1.2 copy-done.1
  2.6 0.0 copy-start.2
  2.6 1.2 copy-done.2
  3.9 0.0 copy-start.3
  3.9 1.2 copy-done.3
  5.1 0.0 copy-start.4
  5.1 60.9 %shard_map.102 = (bf16[32,128,128]{2,1,0:T(8,128)(2,1)S(1)}, bf16[32,256,128]{2,1,0:T(8,128)(2,1)}, bf16[16,256,128]{2,1,0:T(8,128)(2,1)S(1)}, bf16[512,2048]{1,0:T(8,128)(2,1)}) custom-call(bf16[256,2048]{1,0:T(8,128)(2,1)S(1)} %bitcast.16, bf16[256,2048]{1,0:T(8,128)(2,1)S(1)} %bitcast.17, bf16[256,2048]{1,0:T(8,128)(2,1)S(1)} %bitcast.18, ...), custom_call_target="tpu_custom_call" | custom-call | tf_op jit(solution)/shard_map/pallas_call | solution.py:187
  66.0 0.0 copy-done.4
  66.0 39.0 %shard_map.103 = (bf16[4096,128]{1,0:T(8,128)(2,1)S(1)}, bf16[64,8192]{1,0:T(8,128)(2,1)S(1)}, bf16[8192,128]{1,0:T(8,128)(2,1)}) custom-call(s32[64,10]{1,0:T(8,128)S(1)} %bitcast.20, s32[64]{0:T(128)S(1)} %bitcast.21, bf16[4096,128]{1,0:T(8,128)(2,1)S(1)} %bitcast.14, bf16[4096,128]{1,0:T(8,128)(2,1)S(1)} %bitcast.15, bf16[8192,128]{1,0:T(8,128)(2,1)} %bitcast.23), custom_call_target="tpu_custom_call" | custom-call | tf_op jit(solution)/shard_map/pallas_call | solution.py:567
  105.1 100.2 %shard_map.104 = (bf16[32,128,128]{2,1,0:T(8,128)(2,1)S(1)}, bf16[32,256,128]{2,1,0:T(8,128)(2,1)S(1)}, bf16[512,2048]{1,0:T(8,128)(2,1)}) custom-call(bf16[64,8192]{1,0:T(8,128)(2,1)S(1)} %get-tuple-element.21.ot_ref, bf16[32,128,128]{2,1,0:T(8,128)(2,1)S(1)} %bitcast.19, bf16[32,256,128]{2,1,0:T(8,128)(2,1)} %bitcast.22, ...), custom_call_target="tpu_custom_call" | custom-call | tf_op jit(solution)/shard_map/pallas_call | solution.py:404
  205.3 0.0 copy-start
  205.3 1.6 copy-done
  206.9 4.1 %shard_map.105 = (bf16[256,2048]{1,0:T(8,128)(2,1)}, bf16[256,2048]{1,0:T(8,128)(2,1)}, bf16[256,2048]{1,0:T(8,128)(2,1)}, f32[512,2048]{1,0:T(8,128)}) custom-call(bf16[32,128,128]{2,1,0:T(8,128)(2,1)S(1)} %get-tuple-element.25.dq_ref, bf16[32,256,128]{2,1,0:T(8,128)(2,1)S(1)} %get-tuple-element.26.dkv_ref, bf16[512,2048]{1,0:T(8,128)(2,1)S(1)} %copy-done), custom_call_target="tpu_custom_call" | custom-call | tf_op jit(solution)/shard_map/pallas_call | solution.py:441
Async XLA Ops:
  1.4 1.2 copy-start.1
  2.6 1.2 copy-start.2
  3.9 1.2 copy-start.3
  5.1 60.9 %copy-start.4 = (s32[1,64]{1,0:T(1,128)S(1)}, s32[1,64]{1,0:T(1,128)}, u32[]{:S(2)}) copy-start(s32[1,64]{1,0:T(1,128)} %param.13) | copy-start | bytes 772
  205.3 1.6 copy-start

commit v4 on v3

--- a/solution.py
+++ b/solution.py
@@ -18,10 +18,13 @@
 PLANES = 4
 D = 2048
 ROWS = 256
+TRIPLE = BLK + ROWS
 BF = jnp.bfloat16
 F32 = jnp.float32
-GROUPS = (10, 22, 28, 32)
-PARTS = ((0, 768), (768, 640), (1408, 640))
+GROUPS = (20, 32, 32)
+PARTS = ((0, 640), (640, 640), (1280, 384), (1664, 384))
+ORDERS = ((0, 1, 2), (0, 2, 1), (1, 2, 0), (2, 0, 1))
+STEPS = ((2, 0), (3, 0), (2, 1), (3, 1), (0, 0), (1, 0), (2, 2), (3, 2), (0, 1), (1, 1), (0, 2), (1, 2))
 
 
 def remote(src, dst, send_sem, recv_sem, **where):
@@ -72,15 +75,19 @@
             jnp.concatenate([one[:, HD:], two[:, HD:]], axis=1))
 
 
-def head_kernel(q_ref, k_ref, v_ref, og_ref, w_ref, q_out, kv_out, g_out, both_out,
-                q_pack, kv_pack, g_pack, both_ref, w_buf,
-                q_send, kv_send, g_send, q_recv, kv_recv, g_recv,
+def head_kernel(q_ref, k_ref, v_ref, og_ref, w_ref, all_out, g_out, both_out,
+                q_buf, k_buf, v_buf, all_pack, g_pack, both_ref, w_buf,
+                all_send, g_send, all_recv, g_recv, load_sem,
                 w_send, w_recv, w_own, both_send, both_recv, both_own):
     plane, member, chip, core, _, _ = position()
     up, down = lax.rem(plane + 1, PLANES), lax.rem(plane + 3, PLANES)
     far = lax.rem(plane + 2, PLANES)
     sibling = chip * 2 + 1 - core
     mine = pl.ds(pl.multiple_of(core * ROWS, ROWS), ROWS)
+    loads = [local(q_ref, q_buf, load_sem.at[0]), local(k_ref, k_buf, load_sem.at[1]),
+             local(v_ref, v_buf, load_sem.at[2])]
+    for load in loads:
+        load.start()
     w_mine = local(w_ref.at[mine], w_buf.at[plane], w_own.at[0])
     w_mine.start()
     both_mine = local(og_ref, both_ref.at[mine], w_own.at[1])
@@ -110,25 +117,20 @@
     def pair_owner(j, e):
         return traced_owner(lax.div(j, 4), lax.rem(lax.div(j, 2), 2), lax.rem(j, 2) * 2 + e)
 
+    for load in loads:
+        load.wait()
+
     @pl.loop(0, CHIPS)
     def _(k):
         j = lax.rem(chip + 5 * k, CHIPS)
         at = pl.ds(pl.multiple_of(j * 2 * HD, 2 * HD), 2 * HD)
-        kv = halves(k_ref[:, at], v_ref[:, at])
+        q = halves(q_buf[:BLK, at], q_buf[BLK:, at])
+        kv = halves(k_buf[:, at], v_buf[:, at])
         for e in range(2):
             to = pair_owner(j, e)
-            kv_pack[to] = kv[e]
-            send(kv_pack.at[to], to, kv_out, member, kv_send.at[to], kv_recv)
-
-    @pl.loop(0, CHIPS)
-    def _(k):
-        j = lax.rem(chip + 5 * k, CHIPS)
-        at = pl.ds(pl.multiple_of(j * 2 * HD, 2 * HD), 2 * HD)
-        q = halves(q_ref[:BLK, at], q_ref[BLK:, at])
-        for e in range(2):
-            to = pair_owner(j, e)
-            q_pack[to] = q[e]
-            send(q_pack.at[to], to, q_out, member, q_send.at[to], q_recv)
+            all_pack[to, :BLK] = q[e]
+            all_pack[to, BLK:] = kv[e]
+            send(all_pack.at[to], to, all_out, member, all_send.at[to], all_recv)
 
     def project(which):
         for pair in range(2):
@@ -167,53 +169,54 @@
 
     @pl.loop(0, SEQ)
     def _(d):
-        sent(kv_pack.at[d], d, kv_out, member, kv_send.at[d], kv_recv)
-        sent(q_pack.at[d], d, q_out, member, q_send.at[d], q_recv)
+        sent(all_pack.at[d], d, all_out, member, all_send.at[d], all_recv)
 
     @pl.loop(0, CHIPS)
     def _(slot):
         head = traced_owner(lax.div(slot, SIDE), core, lax.rem(slot, SIDE))
         sent(g_pack.at[slot], head, g_out, chip, g_send.at[slot], g_recv)
 
-    local(kv_out, kv_out, kv_recv).wait()
-    local(q_out, q_out, q_recv).wait()
+    local(all_out, all_out, all_recv).wait()
     local(g_out, g_out, g_recv).wait()
 
 
 def head_exchange(queries, keys, values, out_grad, out_weight):
     anyway = pl.BlockSpec(memory_space=pl.ANY)
-    whole = pl.BlockSpec(memory_space=pltpu.VMEM)
     dma = pltpu.SemaphoreType.DMA
     return pl.pallas_call(
         head_kernel,
         out_shape=(
-            jax.ShapeDtypeStruct((SEQ, BLK, 2 * HD), BF),
-            jax.ShapeDtypeStruct((SEQ, ROWS, 2 * HD), BF),
+            jax.ShapeDtypeStruct((SEQ, TRIPLE, 2 * HD), BF),
             jax.ShapeDtypeStruct((CHIPS, ROWS, 2 * HD), BF),
             jax.ShapeDtypeStruct((2 * ROWS, D), BF),
         ),
-        in_specs=[whole, whole, whole, whole, anyway],
-        out_specs=(anyway, anyway, anyway, anyway),
+        in_specs=[pl.BlockSpec(memory_space=pltpu.HBM)] * 5,
+        out_specs=(anyway, anyway, anyway),
         scratch_shapes=[
-            pltpu.VMEM((SEQ, BLK, 2 * HD), BF),
-            pltpu.VMEM((SEQ, ROWS, 2 * HD), BF),
+            pltpu.VMEM((ROWS, D), BF),
+            pltpu.VMEM((ROWS, D), BF),
+            pltpu.VMEM((ROWS, D), BF),
+            pltpu.VMEM((SEQ, TRIPLE, 2 * HD), BF),
             pltpu.VMEM((CHIPS, ROWS, 2 * HD), BF),
             pltpu.VMEM((2 * ROWS, D), BF),
             pltpu.VMEM((PLANES, ROWS, D), BF),
-            dma((SEQ,)), dma((SEQ,)), dma((CHIPS,)), dma, dma, dma,
+            dma((SEQ,)), dma((CHIPS,)), dma, dma, dma((3,)),
             dma((4,)), dma((4,)), dma((2,)), dma, dma, dma,
         ],
         compiler_params=pltpu.CompilerParams(
-            collective_id=0, has_side_effects=True, vmem_limit_bytes=48 << 20),
+            collective_id=0, has_side_effects=True, vmem_limit_bytes=60 << 20),
     )(queries, keys, values, out_grad, out_weight)
 
 
-def tail_kernel(ot_ref, dq_ref, dkv_ref, both_ref, dq_out, dkv_out, wo_out,
-                o_buf, own_buf, *rest):
-    bufs = [rest[6 * t:6 * t + 6] for t in range(3)]
-    (o_send, dq_send, dkv_send, o_recv, dq_recv, dkv_recv, step_send, step_recv,
-     wo_send, wo_recv, wo_own, pass_send, pass_recv) = rest[18:]
+def tail_kernel(ot_ref, all_ref, both_in, all_out, wo_out,
+                both_ref, o_buf, own_buf, *rest):
+    parts = len(PARTS)
+    bufs = [rest[6 * t:6 * t + 6] for t in range(parts)]
+    (o_send, all_send, o_recv, all_recv, step_send, step_recv,
+     wo_send, wo_recv, wo_own, pass_send, pass_recv, load_sem) = rest[6 * parts:]
     plane, member, chip, core, x, y = position()
+    load = local(both_in, both_ref, load_sem)
+    load.start()
     entry_barrier(plane, member)
     slot = lax.rem(y + SIDE - x, SIDE) * SIDE + x
 
@@ -235,17 +238,16 @@
         def _():
             local(src, dst, o_recv).start()
 
-    local(dq_ref.at[member], dq_out.at[member], dq_recv).start()
-    local(dkv_ref.at[member], dkv_out.at[member], dkv_recv).start()
+    local(all_ref.at[member], all_out.at[member], all_recv).start()
 
     def group(low, high):
         @pl.loop(low, high)
         def _(k):
             to = lax.rem(member + 9 * k, SEQ)
-            remote(dkv_ref.at[to], dkv_out.at[member], dkv_send.at[to], dkv_recv, seq=to).start()
-            remote(dq_ref.at[to], dq_out.at[member], dq_send.at[to], dq_recv, seq=to).start()
+            remote(all_ref.at[to], all_out.at[member], all_send.at[to], all_recv, seq=to).start()
 
     group(1, GROUPS[0])
+    load.wait()
     local(o_buf, o_buf, o_recv).wait()
 
     def place(part, zq, value, at):
@@ -257,15 +259,16 @@
             for yq in range(SIDE):
                 piece = value[(xq * SIDE + yq) * 16:(xq * SIDE + yq + 1) * 16]
                 if part == 1:
+                    buf[zq, yq * 64 + xq * 16:yq * 64 + xq * 16 + 16, at] = piece
+                elif part == 2:
                     buf[xq, pl.ds(pl.multiple_of(yq * 64 + zq * 16, 16), 16), at] = piece
                 else:
                     buf[yq, pl.ds(pl.multiple_of(zq * 64 + xq * 16, 16), 16), at] = piece
 
     axes = (("fsdp", plane), ("x", x), ("y", y))
-    orders = ((0, 1, 2), (1, 2, 0), (2, 0, 1))
 
     def steps(part, stage):
-        name, here = axes[orders[part][stage]]
+        name, here = axes[ORDERS[part][stage]]
         send_buf, recv_buf = bufs[part][2 * stage], bufs[part][2 * stage + 1]
         copies = []
         for k in range(1, SIDE):
@@ -301,41 +304,41 @@
                             place(part, zq, value[:, half * BLK:(half + 1) * BLK],
                                   slice(col - base, col - base + BLK))
 
-    multiply((0, 1, 2), (0,))
+    multiply((0, 1, 2), (0, 1))
     start(0, 0)
-    multiply((3, 4, 5), (1, 2))
+    multiply((3, 4), (1,))
     start(1, 0)
-    multiply((6, 7), (2,))
+    multiply((5, 6), (2, 3))
     start(2, 0)
+    multiply((7,), (3,))
+    start(3, 0)
     group(GROUPS[0], GROUPS[1])
 
-    for stage in range(3):
-        for part in range(3):
-            copies, here, send_buf, recv_buf = steps(part, stage)
-            for copy in copies:
-                copy.wait_recv()
-            base, width = PARTS[part]
-            rows = send_buf.shape[1]
-            total = None
-            for piece in range(max(1, rows // 64)):
-                count = min(rows, 64)
-                at = pl.ds(piece * count, count)
-                total = send_buf[here, at, :].astype(F32)
-                for k in range(1, SIDE):
-                    total = total + recv_buf[lax.rem(here + k, SIDE), at, :].astype(F32)
-                if stage == 2:
-                    own_buf[:, base:base + width] = total.astype(BF)
+    for part, stage in STEPS:
+        copies, here, send_buf, recv_buf = steps(part, stage)
+        for copy in copies:
+            copy.wait_recv()
+        base, width = PARTS[part]
+        rows = send_buf.shape[1]
+        for piece in range(max(1, rows // 64)):
+            count = min(rows, 64)
+            at = pl.ds(piece * count, count)
+            total = send_buf[here, at, :].astype(F32)
+            for k in range(1, SIDE):
+                total = total + recv_buf[lax.rem(here + k, SIDE), at, :].astype(F32)
+            if stage == 2:
+                own_buf[:, base:base + width] = total.astype(BF)
+            else:
+                next_buf = bufs[part][2 * stage + 2]
+                if rows == 256:
+                    next_buf[piece] = total.astype(BF)
                 else:
-                    next_buf = bufs[part][2 * stage + 2]
-                    if rows == 256:
-                        next_buf[piece] = total.astype(BF)
-                    else:
-                        for t in range(SIDE):
-                            next_buf[t] = total[t * 16:(t + 1) * 16].astype(BF)
-            if stage < 2:
-                start(part, stage + 1)
+                    for t in range(SIDE):
+                        next_buf[t] = total[t * 16:(t + 1) * 16].astype(BF)
         if stage < 2:
-            group(GROUPS[stage + 1], GROUPS[stage + 2])
+            start(part, stage + 1)
+        if (part, stage) == (3, 0):
+            group(GROUPS[1], GROUPS[2])
 
     def wo_rows(which, q):
         return wo_out.at[pl.ds(pl.multiple_of((which * CHIPS + q) * 16, 16), 16)]
@@ -349,25 +352,31 @@
         q = lax.rem(chip + 5 * k, CHIPS)
         remote(own_buf, wo_rows(core, chip), wo_send.at[q], wo_recv.at[chip], seq=q * 2 + core).start()
 
-    first = remote(own_buf, wo_rows(core, chip), pass_send.at[chip], pass_recv, seq=sibling)
-    first.start()
-
-    @pl.loop(1, CHIPS)
-    def _(k):
-        q = lax.rem(chip + 11 * k, CHIPS)
-        remote(own_buf, wo_rows(core, q), wo_send.at[q], wo_recv.at[q], seq=q * 2 + core).wait_recv()
-        remote(wo_rows(core, q), wo_rows(core, q), pass_send.at[q], pass_recv, seq=sibling).start()
+    def pass_copy(row):
+        rows = wo_out.at[pl.ds(pl.multiple_of((core * CHIPS + row * SIDE) * 16, 64), 64)]
+        return remote(rows, rows, pass_send.at[row], pass_recv, seq=sibling)
 
     own.wait()
+    for k in range(SIDE):
+        row = lax.rem(x + k, SIDE)
+        for t in range(SIDE):
+            q = row * SIDE + lax.rem(y + t, SIDE)
+            if k == 0 and t == 0:
+                continue
+            remote(own_buf, wo_rows(core, q), wo_send.at[q], wo_recv.at[q], seq=q * 2 + core).wait_recv()
+        pass_copy(row).start()
+
     other = pl.ds(pl.multiple_of((1 - core) * ROWS, ROWS), ROWS)
     local(wo_out.at[other], wo_out.at[other], pass_recv).wait()
-    first.wait_send()
+
+    @pl.loop(0, SIDE)
+    def _(row):
+        pass_copy(row).wait_send()
 
     @pl.loop(1, CHIPS)
     def _(k):
         q = lax.rem(chip + k, CHIPS)
         remote(own_buf, wo_rows(core, chip), wo_send.at[q], wo_recv.at[chip], seq=q * 2 + core).wait_send()
-        remote(wo_rows(core, q), wo_rows(core, q), pass_send.at[q], pass_recv, seq=sibling).wait_send()
 
     @pl.loop(0, CHIPS)
     def _(q):
@@ -378,24 +387,20 @@
         def _():
             remote(src, dst, o_send.at[q], o_recv, seq=to).wait_send()
 
-    for stage in range(3):
-        for part in range(3):
-            for copy in steps(part, stage)[0]:
-                copy.wait_send()
+    for part, stage in STEPS:
+        for copy in steps(part, stage)[0]:
+            copy.wait_send()
 
     @pl.loop(1, SEQ)
     def _(k):
         to = lax.rem(member + k, SEQ)
-        remote(dkv_ref.at[to], dkv_out.at[member], dkv_send.at[to], dkv_recv, seq=to).wait_send()
-        remote(dq_ref.at[to], dq_out.at[member], dq_send.at[to], dq_recv, seq=to).wait_send()
-
-    local(dkv_out, dkv_out, dkv_recv).wait()
-    local(dq_out, dq_out, dq_recv).wait()
-
-
-def tail_exchange(ot, dq, dkv, both):
+        remote(all_ref.at[to], all_out.at[member], all_send.at[to], all_recv, seq=to).wait_send()
+
+    local(all_out, all_out, all_recv).wait()
+
+
+def tail_exchange(ot, grads, both):
     anyway = pl.BlockSpec(memory_space=pl.ANY)
-    whole = pl.BlockSpec(memory_space=pltpu.VMEM)
     dma = pltpu.SemaphoreType.DMA
     stages = []
     for _, width in PARTS:
@@ -404,58 +409,76 @@
     return pl.pallas_call(
         tail_kernel,
         out_shape=(
-            jax.ShapeDtypeStruct((SEQ, BLK, 2 * HD), BF),
-            jax.ShapeDtypeStruct((SEQ, ROWS, 2 * HD), BF),
+            jax.ShapeDtypeStruct((SEQ, TRIPLE, 2 * HD), BF),
             jax.ShapeDtypeStruct((2 * ROWS, D), BF),
         ),
-        in_specs=[anyway, anyway, anyway, whole],
-        out_specs=(anyway, anyway, anyway),
+        in_specs=[anyway, anyway, anyway],
+        out_specs=(anyway, anyway),
         scratch_shapes=[
+            pltpu.VMEM((2 * ROWS, D), BF),
             pltpu.VMEM((CHIPS, HD, 2 * ROWS), BF),
             pltpu.VMEM((16, D), BF),
             *stages,
-            dma((CHIPS,)), dma((SEQ,)), dma((SEQ,)), dma, dma, dma,
-            dma((3, 3, 3)), dma((3, 3, 3)),
-            dma((CHIPS,)), dma((CHIPS,)), dma, dma((CHIPS,)), dma,
+            dma((CHIPS,)), dma((SEQ,)), dma, dma,
+            dma((len(PARTS), 3, 3)), dma((len(PARTS), 3, 3)),
+            dma((CHIPS,)), dma((CHIPS,)), dma, dma((SIDE,)), dma, dma,
         ],
         compiler_params=pltpu.CompilerParams(
-            collective_id=1, has_side_effects=True, vmem_limit_bytes=48 << 20),
-    )(ot, dq, dkv, both)
+            collective_id=1, has_side_effects=True, vmem_limit_bytes=60 << 20),
+    )(ot, grads, both)
 
 
 def finish_kernel(dq_ref, dkv_ref, wo_ref, dq_out, dk_out, dv_out, wo_out):
+    step = pl.program_id(0)
     for j in range(HEADS // 2):
         at = slice(j * 2 * HD, (j + 1) * 2 * HD)
-        one, two = dkv_ref[owner(2 * j)], dkv_ref[owner(2 * j + 1)]
-        dk_out[:, at], dv_out[:, at] = halves(one, two)
-        one, two = dq_ref[owner(2 * j)], dq_ref[owner(2 * j + 1)]
-        dq_out[:BLK, at], dq_out[BLK:, at] = halves(one, two)
-    for r in range(8):
-        at = slice(r * 64, (r + 1) * 64)
-        wo_out[at, :] = wo_ref[at, :].astype(F32)
-
-
-def finish(dq, dkv, wo):
-    whole = pl.BlockSpec(memory_space=pltpu.VMEM)
+        one, two = owner(2 * j), owner(2 * j + 1)
+        dk_out[:, at], dv_out[:, at] = halves(dkv_ref[one], dkv_ref[two])
+        low, high = halves(dq_ref[one], dq_ref[two])
+        dq_out[:, at] = jnp.where(step < 2, low, high)
+    wo_out[...] = wo_ref[...].astype(F32)
+
+
+def finish(grads, wo):
+    rows = ROWS // 4
+    packed = (SEQ, rows, 2 * HD)
     shape = jax.ShapeDtypeStruct((ROWS, D), BF)
+    block = pl.BlockSpec((rows, D), lambda r: (r, 0))
+    term = pl.BlockSpec((2 * rows, D), lambda r: (r, 0))
     return pl.pallas_call(
         finish_kernel,
+        grid=(4,),
         out_shape=(shape, shape, shape, jax.ShapeDtypeStruct(wo.shape, F32)),
-        in_specs=[whole] * 3,
-        out_specs=(whole,) * 4,
-        compiler_params=pltpu.CompilerParams(vmem_limit_bytes=48 << 20),
-    )(dq, dkv, wo)
-
-
-def attention_kernel(adj_ref, count_ref, q_ref, g_ref, kv_ref, dq_ref, ot_ref, dkv_ref,
-                     qg_ref, acc_ref, kvt_ref, dqt_ref, sd_ref, te_ref, list_ref, size_ref):
-    blocks = kv_ref.shape[0] // BLK
+        in_specs=[
+            pl.BlockSpec(packed, lambda r: (0, lax.rem(r, 2), 0)),
+            pl.BlockSpec(packed, lambda r: (0, r + 2, 0)),
+            term,
+        ],
+        out_specs=(block, block, block, term),
+        compiler_params=pltpu.CompilerParams(vmem_limit_bytes=60 << 20),
+    )(grads, grads, wo)
+
+
+def attention_kernel(adj_in, count_in, all_ref, g_ref, ot_ref, grads_ref,
+                     qg_ref, acc_ref, kvt_ref, dqt_ref, sd_ref, te_ref, list_ref, size_ref,
+                     adj_ref, count_ref, table_sem):
+    blocks = ot_ref.shape[1] // BLK
+    tables = [pltpu.make_async_copy(adj_in.at[0], adj_ref, table_sem.at[0]),
+              pltpu.make_async_copy(count_in.at[0], count_ref, table_sem.at[1])]
+    for table in tables:
+        table.start()
     first = lax.broadcasted_iota(jnp.int32, (BLK, BLK), 1) < HD
     half_scale = jnp.where(first, HD ** -0.5, 1.0).astype(F32)
     score_scale = HD ** -0.5 * LOG2E
 
     def rows(b):
         return pl.ds(pl.multiple_of(b * BLK, BLK), BLK)
+
+    def kv_rows(b):
+        return pl.ds(pl.multiple_of((b + lax.div(b, 2) + 1) * BLK, BLK), BLK)
+
+    def q_rows(b):
+        return pl.ds(pl.multiple_of(b * TRIPLE, BLK), BLK)
 
     def swap(value):
         return jnp.concatenate([value[:, HD:], value[:, :HD]], axis=1)
@@ -465,15 +488,17 @@
         for t in range(8):
             b = s * 8 + t
             acc_ref[rows(b), :] = jnp.zeros((BLK, BLK), F32)
-            kvt_ref[rows(b), :] = kv_ref[rows(b), :].T
+            kvt_ref[rows(b), :] = all_ref[kv_rows(b), :].T
         for t in range(4):
             b = s * 4 + t
-            q, g = q_ref[rows(b), :], g_ref[rows(b), :]
+            q, g = all_ref[q_rows(b), :], g_ref[rows(b), :]
             qg_ref[rows(2 * b), :] = jnp.where(first, q, swap(g))
             qg_ref[rows(2 * b + 1), :] = jnp.where(first, swap(q), g)
 
     for n in range(MAXK + 1):
         size_ref[n] = 0
+    for table in tables:
+        table.wait()
 
     @pl.loop(0, blocks)
     def _(i):
@@ -504,7 +529,7 @@
             top = None
             for j in range(n):
                 sd = lax.dot_general(
-                    kv_ref[rows(picked[m][j]), :], pairs[m], (((1,), (1,)), ((), ())),
+                    all_ref[kv_rows(picked[m][j]), :], pairs[m], (((1,), (1,)), ((), ())),
                     preferred_element_type=F32)
                 sd_ref[m, slots[j], :] = sd
                 part = fold(sd[:, :BLK], jnp.maximum)
@@ -554,25 +579,24 @@
     def _(s):
         for t in range(8):
             b = s * 8 + t
-            dkv_ref[rows(b), :] = (acc_ref[rows(b), :] * half_scale).astype(BF)
+            grads_ref[kv_rows(b), :] = (acc_ref[rows(b), :] * half_scale).astype(BF)
         for t in range(4):
             b = s * 4 + t
-            dq_ref[rows(b), :] = dqt_ref[rows(b), :].T.astype(BF)
-
-
-def attention(adjacency, counts, q, g, kv):
-    tokens = kv.shape[0]
+            grads_ref[q_rows(b), :] = dqt_ref[rows(b), :].T.astype(BF)
+
+
+def attention(adjacency, counts, tokens_in, g):
+    tokens = 2 * g.shape[0]
     whole = pl.BlockSpec(memory_space=pltpu.VMEM)
-    scalar = pl.BlockSpec(memory_space=pltpu.SMEM)
+    scalar = pl.BlockSpec(memory_space=pltpu.HBM)
     return pl.pallas_call(
         attention_kernel,
         out_shape=(
-            jax.ShapeDtypeStruct((tokens // 2, 2 * HD), BF),
             jax.ShapeDtypeStruct((HD, tokens), BF),
-            jax.ShapeDtypeStruct((tokens, 2 * HD), BF),
+            jax.ShapeDtypeStruct(tokens_in.shape, BF),
         ),
-        in_specs=[scalar, scalar, whole, whole, whole],
-        out_specs=(whole, whole, whole),
+        in_specs=[scalar, scalar, whole, whole],
+        out_specs=(whole, whole),
         scratch_shapes=[
             pltpu.VMEM((tokens, 2 * HD), BF),
             pltpu.VMEM((tokens, 2 * HD), F32),
@@ -582,19 +606,20 @@
             pltpu.VMEM((GROUP, MAXK * BLK, 2 * BLK), BF),
             pltpu.SMEM((MAXK + 1, NBLK), jnp.int32),
             pltpu.SMEM((MAXK + 1,), jnp.int32),
+            pltpu.SMEM((NBLK, MAXK), jnp.int32),
+            pltpu.SMEM((NBLK,), jnp.int32),
+            pltpu.SemaphoreType.DMA((2,)),
         ],
-        compiler_params=pltpu.CompilerParams(vmem_limit_bytes=48 << 20),
-    )(adjacency, counts, q, g, kv)
+        compiler_params=pltpu.CompilerParams(vmem_limit_bytes=60 << 20),
+    )(adjacency, counts, tokens_in, g)
 
 
 def on_device(queries, keys, values, out_grad, out_weight, key_blocks, block_counts):
-    q, kv, g, both = head_exchange(queries[0], keys[0], values[0], out_grad[0], out_weight)
-    dq, ot, dkv = attention(
-        key_blocks[0], block_counts[0], q.reshape(-1, 2 * HD), g.reshape(-1, 2 * HD),
-        kv.reshape(-1, 2 * HD))
-    dq, dkv, wo = tail_exchange(
-        ot, dq.reshape(SEQ, BLK, 2 * HD), dkv.reshape(SEQ, ROWS, 2 * HD), both)
-    query_grad, key_grad, value_grad, wo_grad = finish(dq, dkv, wo)
+    tokens_in, g, both = head_exchange(queries[0], keys[0], values[0], out_grad[0], out_weight)
+    ot, grads = attention(
+        key_blocks, block_counts, tokens_in.reshape(-1, 2 * HD), g.reshape(-1, 2 * HD))
+    grads, wo = tail_exchange(ot, grads.reshape(SEQ, TRIPLE, 2 * HD), both)
+    query_grad, key_grad, value_grad, wo_grad = finish(grads, wo)
     return (query_grad[None], key_grad[None], value_grad[None], wo_grad)
 
 

time: 212 us -> 208 us (0.981)
  local copies, waits for them, and re-layouts: 6.04 us -> 1.39 us
    unnamed x11 -> x1, local copies, waits for them, and re-layouts: 6.04 us -> 1.39 us
where the time goes in v4:
time: 208 us; the launch traced here: 207 us
  Pallas kernels  205 us (99%)
    pallas_call x1, Pallas kernels, tail_exchange(): pl.pallas_call(tail_kernel, out_shape=(jax.ShapeDtypeStruct((SEQ, TRIPLE,...  100 us
    pallas_call x1, Pallas kernels, head_exchange(): pl.pallas_call(head_kernel, out_shape=(jax.ShapeDtypeStruct((SEQ, TRIPLE,...  57.7 us
    pallas_call x1, Pallas kernels, attention(): pl.pallas_call(attention_kernel, out_shape=(jax.ShapeDtypeStruct((HD, tok...  40.6 us
    pallas_call x1, Pallas kernels, finish(): pl.pallas_call(finish_kernel, grid=(4,), out_shape=(shape, shape, shape,...  6.63 us

profile of v4, /device:TPU:1, one launch (start us, length us, event | category | flops | bytes accessed | tf_op | source)
XLA Modules:
  0.0 207.2 jit_solution(16130170205388351243)
XLA Ops:
  0.6 1.4 copy.11.adj_in
  2.0 57.7 %shard_map.102 = (bf16[32,384,128]{2,1,0:T(8,128)(2,1)}, bf16[16,256,128]{2,1,0:T(8,128)(2,1)}, bf16[512,2048]{1,0:T(8,128)(2,1)}) custom-call(bf16[256,2048]{1,0:T(8,128)(2,1)} %bitcast.13, bf16[256,2048]{1,0:T(8,128)(2,1)} %bitcast.14, bf16[256,2048]{1,0:T(8,128)(2,1)} %bitcast.15, bf16[256,2048]{1,0:T(8,128)(2,1)} %bitcast.16, bf16[512,2048]{1,0:T(8,128)(2,1)} %w_ref.1), custom_call_target="tpu_custom_call" | custom-call | tf_op jit(solution)/shard_map/pallas_call | solution.py:186
  59.8 40.6 %shard_map.103 = (bf16[64,8192]{1,0:T(8,128)(2,1)}, bf16[12288,128]{1,0:T(8,128)(2,1)}) custom-call(s32[1,64,10]{2,1,0:T(8,128)} %copy.11.adj_in, s32[1,64]{1,0:T(1,128)} %count_in.1, bf16[12288,128]{1,0:T(8,128)(2,1)} %bitcast.11, bf16[4096,128]{1,0:T(8,128)(2,1)} %bitcast.12), custom_call_target="tpu_custom_call" | custom-call | tf_op jit(solution)/shard_map/pallas_call | solution.py:592
  100.4 100.2 %shard_map.104 = (bf16[32,384,128]{2,1,0:T(8,128)(2,1)}, bf16[512,2048]{1,0:T(8,128)(2,1)}) custom-call(bf16[64,8192]{1,0:T(8,128)(2,1)} %get-tuple-element.17.ot_ref, bf16[32,384,128]{2,1,0:T(8,128)(2,1)} %bitcast.10, bf16[512,2048]{1,0:T(8,128)(2,1)} %get-tuple-element.19.both_in), custom_call_target="tpu_custom_call" | custom-call | tf_op jit(solution)/shard_map/pallas_call | solution.py:409
  200.6 6.6 %shard_map.105 = (bf16[256,2048]{1,0:T(8,128)(2,1)}, bf16[256,2048]{1,0:T(8,128)(2,1)}, bf16[256,2048]{1,0:T(8,128)(2,1)}, f32[512,2048]{1,0:T(8,128)}) custom-call(bf16[32,384,128]{2,1,0:T(8,128)(2,1)} %get-tuple-element.20.dq_ref.dkv_ref, bf16[32,384,128]{2,1,0:T(8,128)(2,1)} %get-tuple-element.20.dq_ref.dkv_ref, bf16[512,2048]{1,0:T(8,128)(2,1)} %get-tuple-element.21.wo_ref), custom_call_target="tpu_custom_call" | custom-call | tf_op jit(solution)/shard_map/pallas_call | solution.py:448

commit v5 on v4

--- a/solution.py
+++ b/solution.py
@@ -10,7 +10,7 @@
 BLK = 128
 MAXK = 10
 NBLK = 64
-GROUP = 2
+SPANS = (3, 2, 1)
 LOG2E = 1.4426950408889634
 SEQ = 32
 SIDE = 4
@@ -22,7 +22,7 @@
 BF = jnp.bfloat16
 F32 = jnp.float32
 GROUPS = (20, 32, 32)
-PARTS = ((0, 640), (640, 640), (1280, 384), (1664, 384))
+PARTS = ((0, 768), (768, 768), (1536, 256), (1792, 256))
 ORDERS = ((0, 1, 2), (0, 2, 1), (1, 2, 0), (2, 0, 1))
 STEPS = ((2, 0), (3, 0), (2, 1), (3, 1), (0, 0), (1, 0), (2, 2), (3, 2), (0, 1), (1, 1), (0, 2), (1, 2))
 
@@ -304,11 +304,11 @@
                             place(part, zq, value[:, half * BLK:(half + 1) * BLK],
                                   slice(col - base, col - base + BLK))
 
-    multiply((0, 1, 2), (0, 1))
+    multiply((0, 1, 2), (0,))
     start(0, 0)
-    multiply((3, 4), (1,))
+    multiply((3, 4, 5), (1,))
     start(1, 0)
-    multiply((5, 6), (2, 3))
+    multiply((6,), (2,))
     start(2, 0)
     multiply((7,), (3,))
     start(3, 0)
@@ -435,7 +435,7 @@
         one, two = owner(2 * j), owner(2 * j + 1)
         dk_out[:, at], dv_out[:, at] = halves(dkv_ref[one], dkv_ref[two])
         low, high = halves(dq_ref[one], dq_ref[two])
-        dq_out[:, at] = jnp.where(step < 2, low, high)
+        dq_out[:, at] = jnp.where(lax.rem(step, 2) == 0, low, high)
     wo_out[...] = wo_ref[...].astype(F32)
 
 
@@ -445,16 +445,17 @@
     shape = jax.ShapeDtypeStruct((ROWS, D), BF)
     block = pl.BlockSpec((rows, D), lambda r: (r, 0))
     term = pl.BlockSpec((2 * rows, D), lambda r: (r, 0))
+    turned = pl.BlockSpec((rows, D), lambda r: (lax.rem(r, 2) * 2 + lax.div(r, 2), 0))
     return pl.pallas_call(
         finish_kernel,
         grid=(4,),
         out_shape=(shape, shape, shape, jax.ShapeDtypeStruct(wo.shape, F32)),
         in_specs=[
-            pl.BlockSpec(packed, lambda r: (0, lax.rem(r, 2), 0)),
+            pl.BlockSpec(packed, lambda r: (0, lax.div(r, 2), 0)),
             pl.BlockSpec(packed, lambda r: (0, r + 2, 0)),
             term,
         ],
-        out_specs=(block, block, block, term),
+        out_specs=(turned, block, block, term),
         compiler_params=pltpu.CompilerParams(vmem_limit_bytes=60 << 20),
     )(grads, grads, wo)
 
@@ -565,15 +566,15 @@
 
     for n in range(2, MAXK + 1):
         size = size_ref[n]
-        whole = lax.div(size, GROUP)
-
-        @pl.loop(0, whole)
-        def _(t):
-            process([list_ref[n, t * GROUP + m] for m in range(GROUP)], n)
-
-        @pl.loop(whole * GROUP, size)
-        def _(t):
-            process([list_ref[n, t]], n)
+        done = 0
+        for span in SPANS:
+            steps = lax.div(size - done, span)
+
+            @pl.loop(0, steps)
+            def _(t, n=n, span=span, done=done):
+                process([list_ref[n, done + t * span + m] for m in range(span)], n)
+
+            done = done + steps * span
 
     @pl.loop(0, blocks // 8)
     def _(s):
@@ -602,8 +603,8 @@
             pltpu.VMEM((tokens, 2 * HD), F32),
             pltpu.VMEM((tokens, 2 * HD), BF),
             pltpu.VMEM((tokens // 2, 2 * HD), F32),
-            pltpu.VMEM((GROUP, MAXK * BLK, 2 * BLK), F32),
-            pltpu.VMEM((GROUP, MAXK * BLK, 2 * BLK), BF),
+            pltpu.VMEM((SPANS[0], MAXK * BLK, 2 * BLK), F32),
+            pltpu.VMEM((SPANS[0], MAXK * BLK, 2 * BLK), BF),
             pltpu.SMEM((MAXK + 1, NBLK), jnp.int32),
             pltpu.SMEM((MAXK + 1,), jnp.int32),
             pltpu.SMEM((NBLK, MAXK), jnp.int32),

time: 208 us -> 202 us (0.971)
  Pallas kernels: 205 us -> 199 us
    pallas_call x1, Pallas kernels: 100 us -> 95.5 us  [tail_exchange(): pl.pallas_call(tail_kernel, out_shape=(jax.ShapeDtypeStruct((SEQ, TRIPLE,...]
where the time goes in v5:
time: 202 us; the launch traced here: 201 us
  Pallas kernels  199 us (99%)
    pallas_call x1, Pallas kernels, tail_exchange(): pl.pallas_call(tail_kernel, out_shape=(jax.ShapeDtypeStruct((SEQ, TRIPLE,...  95.5 us
    pallas_call x1, Pallas kernels, head_exchange(): pl.pallas_call(head_kernel, out_shape=(jax.ShapeDtypeStruct((SEQ, TRIPLE,...  57.7 us
    pallas_call x1, Pallas kernels, attention(): pl.pallas_call(attention_kernel, out_shape=(jax.ShapeDtypeStruct((HD, tok...  39 us
    pallas_call x1, Pallas kernels, finish(): pl.pallas_call(finish_kernel, grid=(4,), out_shape=(shape, shape, shape,...  6.59 us

profile of v5, /device:TPU:1, one launch (start us, length us, event | category | flops | bytes accessed | tf_op | source)
XLA Modules:
  0.0 200.9 jit_solution(8226317736547003788)
XLA Ops:
  0.6 1.4 copy.11.adj_in
  2.0 57.7 %shard_map.102 = (bf16[32,384,128]{2,1,0:T(8,128)(2,1)}, bf16[16,256,128]{2,1,0:T(8,128)(2,1)}, bf16[512,2048]{1,0:T(8,128)(2,1)}) custom-call(bf16[256,2048]{1,0:T(8,128)(2,1)} %bitcast.13, bf16[256,2048]{1,0:T(8,128)(2,1)} %bitcast.14, bf16[256,2048]{1,0:T(8,128)(2,1)} %bitcast.15, bf16[256,2048]{1,0:T(8,128)(2,1)} %bitcast.16, bf16[512,2048]{1,0:T(8,128)(2,1)} %w_ref.1), custom_call_target="tpu_custom_call" | custom-call | tf_op jit(solution)/shard_map/pallas_call | solution.py:186
  59.8 39.0 %shard_map.103 = (bf16[64,8192]{1,0:T(8,128)(2,1)}, bf16[12288,128]{1,0:T(8,128)(2,1)}) custom-call(s32[1,64,10]{2,1,0:T(8,128)} %copy.11.adj_in, s32[1,64]{1,0:T(1,128)} %count_in.1, bf16[12288,128]{1,0:T(8,128)(2,1)} %bitcast.11, bf16[4096,128]{1,0:T(8,128)(2,1)} %bitcast.12), custom_call_target="tpu_custom_call" | custom-call | tf_op jit(solution)/shard_map/pallas_call | solution.py:593
  98.8 95.5 %shard_map.104 = (bf16[32,384,128]{2,1,0:T(8,128)(2,1)}, bf16[512,2048]{1,0:T(8,128)(2,1)}) custom-call(bf16[64,8192]{1,0:T(8,128)(2,1)} %get-tuple-element.17.ot_ref, bf16[32,384,128]{2,1,0:T(8,128)(2,1)} %bitcast.10, bf16[512,2048]{1,0:T(8,128)(2,1)} %get-tuple-element.19.both_in), custom_call_target="tpu_custom_call" | custom-call | tf_op jit(solution)/shard_map/pallas_call | solution.py:409
  194.3 6.6 %shard_map.105 = (bf16[256,2048]{1,0:T(8,128)(2,1)}, bf16[256,2048]{1,0:T(8,128)(2,1)}, bf16[256,2048]{1,0:T(8,128)(2,1)}, f32[512,2048]{1,0:T(8,128)}) custom-call(bf16[32,384,128]{2,1,0:T(8,128)(2,1)} %get-tuple-element.20.dq_ref.dkv_ref, bf16[32,384,128]{2,1,0:T(8,128)(2,1)} %get-tuple-element.20.dq_ref.dkv_ref, bf16[512,2048]{1,0:T(8,128)(2,1)} %get-tuple-element.21.wo_ref), custom_call_target="tpu_custom_call" | custom-call | tf_op jit(solution)/shard_map/pallas_call | solution.py:449
